TPU v7x, 32 devices: a whole 2x2x4 slice. The times are simulated.
32 devices in a mesh: gx: 4 (over x, core), gy: 2 (over y), gz: 4 (over z).
Axes of the slice: x: 2, y: 2, z: 4, core: 2. Of those that a mesh axis runs over, the one named last changes fastest.
Arguments:
- features: bfloat16 [32, 64, 32, 512], P(None, 'gx', 'gy', 'gz'), may hold values from -6 to 6
- weight: bfloat16 [27, 32], replicated, may hold values from -0.21875 to 0.21875
- bias: float32 [1], replicated, may hold values from -2 to 2
- label: int32 [64, 32, 512], P('gx', 'gy', 'gz'), may hold values from 0 to 1, as said below
Outputs:
- loss: float32 [1], replicated
- grad_features: bfloat16 [32, 64, 32, 512], P(None, 'gx', 'gy', 'gz')
- grad_weight: float32 [27, 32], replicated
- grad_bias: float32 [1], replicated
Inputs may be any that keep to these rules, and one draw needn't show every extreme that they name: label is 1 at vessel voxels and 0 elsewhere.
All inputs are finite; a program needn't handle non-finite values.
Results may differ from a plain program's by a relative error of at most 0.005.
Values may be sent and summed in bfloat16 or wider, within the bound.
No kernel may reach another device: no remote copies, remote signals or barrier semaphores. Data moves between devices by JAX's collectives and lax.ppermute only.
A program may use at most 128 MiB of HBM per device.

v0:
```python
import functools

import jax
import jax.numpy as jnp
from jax import lax
from jax.experimental import pallas as pl
from jax.experimental.pallas import tpu as pltpu
from jax.sharding import PartitionSpec as P

ITERS = 10
SECTIONS = ITERS + 1
LANES = 128
HALO = SECTIONS + 2
BACK = SECTIONS + 1

BLOCK = 32
SPAN_BLOCK = 40
ERODE_BLOCK = 20

temper = 20.0
sharpness = 40.0

GROUP = ("gx", "gy")
ALL_AXES = ("gx", "gy", "gz")
f32 = jnp.float32
bf16 = jnp.bfloat16


def up8(value):
    return -(-value // 8) * 8


class Plan:
    def __init__(self, mesh_shape, block):
        self.ch, self.nx, self.ny, self.nz = block
        self.gx, self.gy, self.gz = (mesh_shape[a] for a in ALL_AXES)
        self.members = self.gx * self.gy
        self.ranks = self.members * self.gz
        self.X = self.nx * self.gx
        self.Y = self.ny * self.gy
        self.Z = self.nz * self.gz
        assert LANES % self.Y == 0 and self.nz == LANES
        assert self.nz % self.members == 0
        self.zc = self.nz // self.members
        self.per = LANES // self.Y
        assert self.nx % self.per == 0
        self.tiles = self.X // self.per
        self.own = self.nx // self.per
        self.shared = self.per > 1
        self.sent = self.own + (1 if self.shared else 2)
        self.R = up8(self.zc)
        self.extra = -(-2 * self.sent // self.R)
        self.R16 = -(-self.zc // 16) * 16
        self.extra16 = -(-2 * self.sent // self.R16)
        self.pad = self.tiles + 16
        self.win = self.zc + 2 * HALO
        self.span = self.zc + 2
        self.block = self.blocks_of(self.zc, BLOCK)
        self.span_block = self.blocks_of(self.span, SPAN_BLOCK)
        self.win_block = self.blocks_of(self.win, 32)
        self.erode_block = max(1, ERODE_BLOCK * 8 // self.tiles)
        self.base = HALO + 1
        self.planes = self.zc + 2 * HALO + 2 + self.erode_block
        self.pull_base = BACK + 2
        self.pull_planes = self.zc + 2 * BACK + 4 + self.erode_block
        self.hops = -(-HALO // self.zc)
        self.rest = HALO - (self.hops - 1) * self.zc
        self.records = 3 * self.zc + self.span
        assert self.ny == 16 and self.gy > 1
        self.back_hops = -(-(BACK + 1) // self.zc)

    def back_count(self, h):
        return min(self.zc + BACK + 1 - h * self.zc, self.span)

    def blocks_of(self, count, most):
        fits = [n for n in range(1, count + 1) if count % n == 0 and n * self.tiles <= 8 * most]
        return fits[-1] if fits else 1

    def slab(self, member):
        x, y = member // self.gy, member % self.gy
        return y * self.gx + (x if y % 2 == 0 else self.gx - 1 - x)

    def member(self, slab, odd):
        slab = self.members - 1 - slab if odd else slab
        return next(p for p in range(self.members) if self.slab(p) == slab)

    def member_now(self, slab, pos_ref):
        odd = pos_ref[0] // self.members % 2 == 1
        return jnp.where(odd, self.member(slab, True), self.member(slab, False))

    def label_lane(self, member_y):
        return 0 if member_y == self.gy - 1 else (member_y + 1) * self.ny + 8

    def slot(self, x):
        if 0 <= x < self.nx:
            return x // self.per, (x % self.per) * self.Y
        if x == self.nx:
            return self.own, 0
        return self.sent - 1, LANES - self.Y


def lane_iota(shape):
    return lax.broadcasted_iota(jnp.int32, shape, len(shape) - 1)


def row_iota(shape):
    return lax.broadcasted_iota(jnp.int32, shape, len(shape) - 2)


def masks(plan):
    return lane_iota((plan.tiles, LANES))


def x_neighbours(plan, mask, load, cur):
    lower, upper = load(-1), load(1)
    if plan.Y == LANES:
        return lower + upper
    lower = pltpu.roll(jnp.where(mask >= LANES - plan.Y, lower, cur), plan.Y, 1)
    upper = pltpu.roll(jnp.where(mask < plan.Y, upper, cur), LANES - plan.Y, 1)
    return lower + upper


def y_matrix(plan, ref):
    row = row_iota((2 * LANES, LANES)) % LANES
    lane = lane_iota((2 * LANES, LANES))
    near = (row == lane - 1) | (row == lane + 1)
    ref[...] = (near & (row // plan.Y == lane // plan.Y)).astype(f32).astype(bf16)


def y_neighbours(ref, block):
    flat = block.reshape(-1, LANES)
    high = flat.astype(bf16)
    low = (flat - high.astype(f32)).astype(bf16)
    both = jnp.concatenate([high, low], axis=1)
    return jnp.dot(both, ref[...], preferred_element_type=f32).reshape(block.shape)


def count_tables(plan, cross_ref, box_ref):
    flat = row_iota((plan.tiles, LANES)) * LANES + lane_iota((plan.tiles, LANES))
    y, x = flat % plan.Y, flat // plan.Y

    def along(spot, size):
        return 3.0 - (spot == 0).astype(f32) - (spot == size - 1).astype(f32)

    cx, cy = along(x, plan.X), along(y, plan.Y)
    for kind, cz in ((1, 2.0), (2, 3.0)):
        if cross_ref is not None:
            cross_ref[kind] = 1.0 / (cx + cy + cz - 2.0)
        if box_ref is not None:
            box_ref[kind] = 1.0 / (cx * cy * cz)
    for ref in (cross_ref, box_ref):
        if ref is not None:
            ref[0] = jnp.zeros((plan.tiles, LANES), f32)


def kind_of(plan, rank, plane):
    z = rank * plan.zc + plane
    inside = (z >= 0) & (z < plan.Z)
    edge = (z == 0) | (z == plan.Z - 1)
    return jnp.where(inside, jnp.where(edge, 1, 2), 0), jnp.where(inside, 0.0, 1.0)


def store_all(pairs):
    for ref, at, value in pairs:
        ref[at] = value


def over(first, count, size, body):
    def at(n, carry):
        body(first + n * size)
        return carry

    lax.fori_loop(0, (count + size - 1) // size, at, 0)


def tap_condition(plan, member_y, shape, y_dim, in_dim):
    y = lax.broadcasted_iota(jnp.int32, shape, y_dim) % plan.Y
    own = lax.broadcasted_iota(jnp.int32, shape, in_dim) % plan.ny
    return own + member_y * plan.ny - y + 1


PARTS = 4


def stream(plan, far_ref, near_ref, sem_ref):
    width = plan.nx // PARTS
    copies = []
    for n in range(PARTS):
        span = pl.ds(n * width, width)
        copies.append(
            pltpu.make_async_copy(far_ref.at[:, span], near_ref.at[:, span], sem_ref.at[n])
        )
        copies[-1].start()
    return copies


def columns(plan, ref, first, count):
    blocks = [ref[:, x].reshape(-1, plan.nz) for x in range(first, first + count)]
    return jnp.concatenate(blocks, axis=1)


def moved_columns(ref, first, count):
    blocks = [
        jnp.concatenate([ref[x + 2], ref[x + 1], ref[x]], axis=0)
        for x in range(first, first + count)
    ]
    return jnp.concatenate(blocks, axis=1)


def conv_kernel(
    plan, pos_ref, w_ref, far_ref, label_ref, out_ref, wide_ref, acc_ref, f_ref, sem_ref
):
    width = plan.nx // PARTS
    copies = stream(plan, far_ref, f_ref, sem_ref)
    rows, inner = plan.Y, plan.ch * plan.ny
    spread = (
        lax.broadcasted_iota(jnp.int32, (plan.ch, inner), 0)
        == lax.broadcasted_iota(jnp.int32, (plan.ch, inner), 1) // plan.ny
    )
    taps = jnp.dot(
        w_ref[...], spread.astype(f32).astype(bf16), preferred_element_type=f32
    )
    tap_y = tap_condition(plan, pos_ref[1], (rows, inner), 0, 1)
    for i in range(3):
        for k in range(3):
            band = jnp.zeros((rows, inner), f32)
            for j in range(3):
                t = 9 * i + 3 * j + k
                band = jnp.where(tap_y == j, taps[t : t + 1], band)
            at = (3 * i + k) * rows
            wide_ref[at : at + rows] = band.astype(bf16)
    acc_ref[...] = jnp.zeros_like(acc_ref)

    for n in range(PARTS):
        copies[n].wait()
        first = n * width
        out = jnp.dot(
            wide_ref[...], columns(plan, f_ref, first, width), preferred_element_type=f32
        )
        for slot in range(first, first + width + 2):
            terms = [
                out[3 * i * rows : 3 * (i + 1) * rows, (x - first) * plan.nz : (x - first + 1) * plan.nz]
                for i in range(3)
                for x in (slot - 2 + i,)
                if first <= x < first + width
            ]
            acc_ref[slot] += functools.reduce(jnp.add, terms)

    out_ref[...] = jnp.zeros_like(out_ref)
    places = {}
    for x in range(-1, plan.nx + 1):
        tile, lane = plan.slot(x)
        places.setdefault(tile, {})[lane] = x
    lane = lane_iota((rows, plan.nz))
    words = [label_ref[x, 0:8] + 2 * label_ref[x, 8:16] for x in range(plan.nx)]
    first_group = jnp.where(
        pos_ref[1] == plan.gy - 1, 0, (pos_ref[1] + 1) * (plan.ny // 8) + 1
    )
    labelled = lax.broadcasted_iota(jnp.int32, (rows, plan.nz), 0) // 8 == first_group
    for tile in range(plan.sent):
        parts, spills = [], []
        for first in range(0, LANES, rows):
            x = places[tile].get(first)
            if x is None:
                parts.append(jnp.zeros((rows, plan.nz), f32))
                spills.append(jnp.zeros((rows, plan.nz), f32))
                continue
            low = acc_ref[x + 1, 0:rows]
            mid = acc_ref[x + 1, rows : 2 * rows]
            high = acc_ref[x + 1, 2 * rows : 3 * rows]
            total = mid + jnp.where(lane == 0, 0.0, pltpu.roll(low, 1, 1))
            total = total + jnp.where(lane == plan.nz - 1, 0.0, pltpu.roll(high, plan.nz - 1, 1))
            if 0 <= x < plan.nx:
                word = jnp.concatenate([words[x].astype(f32)] * (rows // 8), axis=0)
                total = total + jnp.where(labelled, word, 0.0)
            parts.append(total)
            spill = jnp.where(lane == 1, pltpu.roll(low, 2, 1), 0.0)
            spills.append(jnp.where(lane == 0, high, spill))
        turned = jnp.concatenate(parts, axis=0).T
        spill = jnp.concatenate(spills, axis=0).T
        for j in range(plan.members):
            p = plan.member_now(j, pos_ref)
            out_ref[p, tile, 0 : plan.zc] = turned[j * plan.zc : (j + 1) * plan.zc]
        for end, j in ((0, 0), (1, plan.members - 1)):
            n = 2 * tile + end
            at = plan.sent + n // plan.R
            p = plan.member_now(j, pos_ref)
            out_ref[p, at, n % plan.R : n % plan.R + 1] = spill[end : end + 1]


def gather_kernel(plan, got_ref, out_ref, label_ref, head_ref, tail_ref):
    tiles, zc, rest = plan.tiles, plan.zc, plan.rest
    lane = lane_iota((1, LANES))
    spot = lane % plan.Y

    def part(p, q):
        values = [got_ref[p, q, 0:zc]]
        for end in range(2):
            n = 2 * q + end
            at = plan.sent + n // plan.R
            values.append(got_ref[p, at, n % plan.R : n % plan.R + 1])
        return values

    for a in range(plan.gx):
        for q in range(plan.own):
            parts = []
            label = jnp.zeros((zc, LANES), f32)
            for b in range(plan.gy):
                start = b * plan.ny
                values = part(a * plan.gy + b, q)
                second = (values[0] >= 1.5).astype(f32)
                first = values[0] - 2.0 * second
                move = start - plan.label_lane(b)
                first = pltpu.roll(first, move % LANES, 1)
                second = pltpu.roll(second, (move + 8) % LANES, 1)
                label = jnp.where((spot >= start) & (spot < start + 8), first, label)
                label = jnp.where((spot >= start + 8) & (spot < start + 16), second, label)
                mine = (spot >= start - 1) & (spot <= start + plan.ny)
                parts.append([jnp.where(mine, v, 0.0) for v in values])
                if q == plan.own - 1 and a < plan.gx - 1:
                    edge = part((a + 1) * plan.gy + b, plan.sent - 1)
                    parts.append([jnp.where(lane >= LANES - plan.Y, v, 0.0) for v in edge])
                if q == 0 and a > 0:
                    edge = part((a - 1) * plan.gy + b, plan.own)
                    parts.append([jnp.where(lane < plan.Y, v, 0.0) for v in edge])
            whole, low, high = (functools.reduce(jnp.add, vs) for vs in zip(*parts))
            tile = a * plan.own + q
            label_ref[pl.ds(tile, zc, stride=tiles)] = label
            out_ref[pl.ds(tile, zc, stride=tiles)] = whole
            out_ref[zc * tiles + tile : zc * tiles + tile + 1] = low
            out_ref[(zc + 1) * tiles + tile : (zc + 1) * tiles + tile + 1] = high

    def pack(ref, at, first, count):
        half = -(-count // 2)
        for n in range(half):
            word = label_ref[(first + n) * tiles : (first + n + 1) * tiles]
            if n + half < count:
                other = first + n + half
                word = word + 2.0 * label_ref[other * tiles : (other + 1) * tiles]
            ref[(at + n) * tiles : (at + n + 1) * tiles] = word

    pack(out_ref, zc + 2, 0, zc)
    head_ref[: rest * tiles] = out_ref[: rest * tiles]
    head_ref[rest * tiles : (rest + 1) * tiles] = out_ref[zc * tiles : (zc + 1) * tiles]
    pack(head_ref, rest + 1, 0, rest)
    tail_ref[: rest * tiles] = out_ref[(zc - rest) * tiles : zc * tiles]
    tail_ref[rest * tiles : (rest + 1) * tiles] = out_ref[(zc + 1) * tiles : (zc + 2) * tiles]
    pack(tail_ref, rest + 1, zc - rest, rest)


LOG = 1.0 / sharpness


def thin(e, box, inverse, outside):
    box = box + outside
    ratio = e * box * inverse + outside
    square = ratio * ratio
    more = 1.0 + square
    joint = 1.0 / (box * more)
    slope = joint * box
    return joint * more, slope, jnp.log(square * slope)


def lift(scaled, s):
    small = jnp.exp(scaled * (s - 1.0))
    more = 1.0 + small
    return s + jnp.log(more) * LOG, small * (1.0 / more)


def erode(plan, rank, mask, y_ref, source, result, grown_ref, table_ref, base, first, count):
    tiles = slice(8, 8 + plan.tiles)

    def body(plane):
        beside = y_neighbours(y_ref, source[pl.ds(plane + base, plan.erode_block), tiles])
        for n in range(plan.erode_block):
            at = plane + n + base
            cur = source[at, tiles]

            def load(offset, at=at):
                return source[at, 8 + offset : 8 + offset + plan.tiles]

            total = cur + source[at - 1, tiles] + source[at + 1, tiles]
            total = total + x_neighbours(plan, mask, load, cur) + beside[n]
            kind, outside = kind_of(plan, rank, plane + n)
            total = total * table_ref[kind]
            result[at, tiles] = total
            grown_ref[at] = 1.0 / (total + outside) - outside

    over(first, count, plan.erode_block, body)


def spread(plan, y_ref, grown_ref, zy_ref, base, first, count, size):
    tiles = slice(8, 8 + plan.tiles)

    def body(plane):
        at = plane + base
        part = grown_ref[pl.ds(at - 1, size)] + grown_ref[pl.ds(at, size)]
        part = part + grown_ref[pl.ds(at + 1, size)]
        zy_ref[pl.ds(plane - first, size), tiles] = part + y_neighbours(y_ref, part)

    over(first, count, size, body)


def in_turn(section):
    section(0, 0, 1, True)

    def pair(n, carry):
        section(2 * n + 1, 1, 0, False)
        section(2 * n + 2, 0, 1, False)
        return carry

    lax.fori_loop(0, ITERS // 2, pair, 0)


def x_box(plan, mask, zy_ref, at):
    cur = zy_ref[at, 8 : 8 + plan.tiles]

    def load(offset):
        return zy_ref[at, 8 + offset : 8 + offset + plan.tiles]

    return cur + x_neighbours(plan, mask, load, cur)


def target_kernel(plan, *refs):
    hops = plan.hops
    pos_ref, p_ref, own_ref = refs[:3]
    below, above = refs[3 : 3 + hops], refs[3 + hops : 3 + 2 * hops]
    target_ref, ts_ref, sums_ref = refs[3 + 2 * hops : 6 + 2 * hops]
    all_ref, e0_ref, e1_ref, g_ref, zy_ref, cross_ref, box_ref, y_ref = refs[6 + 2 * hops :]
    zc, win, span = plan.zc, plan.win, plan.span
    size = plan.span_block
    base = HALO + 1
    tiles = slice(8, 8 + plan.tiles)
    rank = pos_ref[0]
    mask = masks(plan)
    count_tables(plan, cross_ref, box_ref)
    y_matrix(plan, y_ref)
    e_refs = (e0_ref, e1_ref)
    e0_ref[...] = jnp.zeros_like(e0_ref)
    e1_ref[...] = jnp.zeros_like(e1_ref)
    zy_ref[...] = jnp.zeros_like(zy_ref)
    all_ref[HALO : HALO + zc] = own_ref[...]
    for h in range(1, hops + 1):
        count = zc if h < hops else plan.rest
        at = zc + 2 if h < hops else plan.rest + 1
        half = -(-count // 2)
        for refs_of, first in ((below, HALO - (h - 1) * zc - count), (above, HALO + h * zc)):
            words = refs_of[h - 1][at : at + half]
            second = (words >= 1.5).astype(f32)
            all_ref[first : first + half] = words - 2.0 * second
            if count > half:
                all_ref[first + half : first + count] = second[: count - half]
    target_ref[...] = all_ref[HALO - 1 : HALO + zc + 1]

    def fill(plane):
        out = []
        for n in range(plan.win_block):
            at = plane + n
            inside = 1.0 - kind_of(plan, rank, at - HALO)[1]
            out.append((e0_ref, (at + 1, tiles), jnp.exp(-temper * all_ref[at]) * inside))
        store_all(out)

    over(0, win, plan.win_block, fill)

    def section(step, source, result, opening):
        e_ref = e_refs[source]
        reach = 2 + ITERS - step
        count = zc + 2 * reach
        erode(
            plan, rank, mask, y_ref, e_ref, e_refs[result], g_ref, cross_ref, base, -reach, count
        )
        spread(plan, y_ref, g_ref, zy_ref, base, -1, span, size)

        def point(plane):
            before = [None if opening else ts_ref[plane + n] for n in range(size)]
            for n in range(size):
                at = plane + n
                box = x_box(plan, mask, zy_ref, at)
                kind, outside = kind_of(plan, rank, at - 1)
                _, _, scaled = thin(e_ref[at - 1 + base, tiles], box, box_ref[kind], outside)
                ts_ref[at] = scaled * -LOG if opening else lift(scaled, before[n])[0]

        over(0, span, size, point)

    in_turn(section)

    def add(n, totals):
        ts = ts_ref[1 + n]
        return totals[0] + ts * p_ref[1 + n], totals[1] + ts

    zero = jnp.zeros((plan.tiles, LANES), f32)
    put_sums(plan, sums_ref, lax.fori_loop(0, zc, add, (zero,) * 2))


def put_sums(plan, ref, totals):
    lines = [jnp.sum(total, axis=0, keepdims=True) for total in totals]
    lines += [jnp.zeros((1, LANES), f32)] * (8 - len(lines))
    ref[...] = jnp.broadcast_to(jnp.concatenate(lines, axis=0)[None], (plan.ranks, 8, LANES))


def get_sums(ref, count):
    lines = jnp.sum(jnp.sum(ref[...], axis=0), axis=1, keepdims=True)
    return [lines[n : n + 1] for n in range(count)]


def forward_kernel(plan, *refs):
    hops = plan.hops
    pos_ref, bias_ref, label_ref, own_ref = refs[:4]
    refs = refs[4:]
    below, above = refs[:hops], refs[hops : 2 * hops]
    refs = refs[2 * hops :]
    far_ref, p_ref, sums_ref = refs[:3]
    e0_ref, e1_ref, g0_ref, g1_ref, zy_ref, s_ref, cross_ref, box_ref = refs[3:11]
    y_ref, record_ref, sem_ref = refs[11:]
    e_refs, g_refs = (e0_ref, e1_ref), (g0_ref, g1_ref)
    base, zc, size = plan.base, plan.zc, plan.block
    tiles = slice(8, 8 + plan.tiles)
    rank = pos_ref[0]
    mask = masks(plan)

    for ref in e_refs + g_refs:
        ref[...] = jnp.zeros_like(ref)
    zy_ref[...] = jnp.zeros_like(zy_ref)
    count_tables(plan, cross_ref, box_ref)
    y_matrix(plan, y_ref)
    e0_ref[base : base + zc, tiles] = own_ref[:zc]
    for h in range(1, hops + 1):
        n = zc if h < hops else plan.rest
        first = base - (h - 1) * zc - n
        e0_ref[first : first + n, tiles] = below[h - 1][:n]
        first = base + h * zc
        e0_ref[first : first + n, tiles] = above[h - 1][:n]
    e0_ref[base - 1, tiles] += own_ref[zc]
    e0_ref[base + zc, tiles] += own_ref[zc + 1]
    for h in range(1, hops + 1):
        if h < hops:
            e0_ref[base - h * zc - 1, tiles] += below[h - 1][zc]
            e0_ref[base + (h + 1) * zc, tiles] += above[h - 1][zc + 1]
            e0_ref[base - (h - 1) * zc, tiles] += below[h - 1][zc + 1]
            e0_ref[base + h * zc - 1, tiles] += above[h - 1][zc]
        else:
            e0_ref[base - (h - 1) * zc, tiles] += below[h - 1][plan.rest]
            e0_ref[base + h * zc - 1, tiles] += above[h - 1][plan.rest]

    def sigmoid(logits):
        small = jnp.exp(-jnp.abs(logits))
        part = 1.0 / (1.0 + small)
        return jnp.where(logits >= 0, part, small * part)

    for n in range(plan.span):
        p_ref[n] = sigmoid(e0_ref[base - 1 + n, tiles] + bias_ref[0])

    def fill(plane):
        out = []
        for n in range(plan.erode_block):
            at = plane + n
            inside = 1.0 - kind_of(plan, rank, at - base)[1]
            predict = sigmoid(e0_ref[at, tiles] + bias_ref[0])
            out.append((e0_ref, (at, tiles), jnp.exp(-temper * predict) * inside))
            out.append((g0_ref, at, jnp.exp(temper * predict) * inside))
        store_all(out)

    over(1, zc + 2 * HALO, plan.erode_block, fill)


    def out_copy(step):
        return pltpu.make_async_copy(record_ref.at[step], far_ref.at[step], sem_ref.at[step])

    def section(step, source, result, opening):
        e_ref, g_ref, after_ref = e_refs[source], g_refs[source], g_refs[result]
        reach = 1 + ITERS - step
        count = zc + 2 * reach
        erode(
            plan, rank, mask, y_ref, e_ref, e_refs[result], after_ref, cross_ref, base, -reach,
            count,
        )
        spread(plan, y_ref, after_ref, zy_ref, base, 0, zc, size)
        record_ref[step, 3 * zc :] = after_ref[base - 1 : base + zc + 1]

        def point(plane):
            before = [None if opening else s_ref[plane + n] for n in range(size)]
            for n in range(size):
                at = plane + n
                box = x_box(plan, mask, zy_ref, at)
                kind, outside = kind_of(plan, rank, at)
                e = e_ref[at + base, tiles]
                over_box, slope, scaled = thin(e, box, box_ref[kind], outside)
                if opening:
                    grown, a = scaled * -LOG, slope
                    record_ref[step, at] = jnp.ones_like(a)
                else:
                    s = before[n]
                    grown, rate = lift(scaled, s)
                    a = rate * (1.0 - s) * slope
                    record_ref[step, at] = 1.0 + rate * scaled * LOG
                s_ref[at] = grown
                record_ref[step, at + zc] = a * over_box
                record_ref[step, at + 2 * zc] = a * g_ref[at + base]

        over(0, zc, size, point)
        out_copy(step).start()

    in_turn(section)

    def add(n, totals):
        ps, predict, target = s_ref[n], p_ref[1 + n], label_ref[n]
        terms = (ps * target, ps, predict * target, predict, target)
        return tuple(total + term for total, term in zip(totals, terms))

    zero = jnp.zeros((plan.tiles, LANES), f32)
    put_sums(plan, sums_ref, lax.fori_loop(0, zc, add, (zero,) * 5))

    def drain(step, carry):
        out_copy(step).wait()
        return carry

    lax.fori_loop(0, SECTIONS, drain, 0)


def backward_kernel(plan, *refs):
    hops = plan.back_hops
    pos_ref, sums_ref, label_ref, far_ref, mine_ref = refs[:5]
    up, down = refs[5 : 5 + hops], refs[5 + hops : 5 + 2 * hops]
    w_ref, push_ref, wt_ref, zy_ref, pull0_ref, pull1_ref, cross_ref = refs[5 + 2 * hops : -3]
    y_ref, record_ref, sem_ref = refs[-3:]
    pull_refs = (pull0_ref, pull1_ref)
    rank = pos_ref[0]
    zc, base = plan.zc, plan.pull_base
    tiles = slice(8, 8 + plan.tiles)
    mask = masks(plan)

    def in_copy(left):
        return pltpu.make_async_copy(far_ref.at[left], record_ref.at[left], sem_ref.at[left])

    for left in reversed(range(SECTIONS)):
        in_copy(left).start()
    s1, s2 = get_sums(sums_ref, 2)
    prec = (s1 + 1.0) / (s2 + 1.0)
    push_ref[...] = jnp.zeros_like(push_ref)
    wt_ref[...] = jnp.zeros_like(wt_ref)
    zy_ref[...] = jnp.zeros_like(zy_ref)
    for ref in pull_refs:
        ref[...] = jnp.zeros_like(ref)
    count_tables(plan, cross_ref, None)
    y_matrix(plan, y_ref)
    w_ref[...] = label_ref[...] - prec[None]

    def section(step, source, result, ending):
        pull_ref, next_ref = pull_refs[source], pull_refs[result]
        left = SECTIONS - 1 - step
        in_copy(left).wait()

        def push(at):
            out = []
            for n in range(plan.block):
                w = w_ref[at + n]
                out.append((push_ref, at + n + 2, w * record_ref[left, at + n + zc]))
                out.append((wt_ref, at + n + base, w * record_ref[left, at + n + 2 * zc]))
                out.append((w_ref, at + n, w * record_ref[left, at + n]))
            store_all(out)

        over(0, zc, plan.block, push)

        def widen(at):
            size = plan.span_block
            part = push_ref[pl.ds(at, size)] + push_ref[pl.ds(at + 1, size)]
            part = part + push_ref[pl.ds(at + 2, size)]
            zy_ref[pl.ds(at, size), tiles] = part + y_neighbours(y_ref, part)

        over(0, plan.span, plan.span_block, widen)

        def pull(at):
            out = []
            for n in range(plan.span_block):
                box = x_box(plan, mask, zy_ref, at + n)
                inverse = cross_ref[kind_of(plan, rank, at + n - 1)[0]]
                grown = record_ref[left, at + n + 3 * zc]
                spot = at + n - 1 + base
                old = pull_ref[spot, tiles]
                out.append((pull_ref, (spot, tiles), old - grown * grown * box * inverse))
            store_all(out)

        over(0, plan.span, plan.span_block, pull)
        reach = 2 + step

        def join(plane):
            beside = y_neighbours(y_ref, pull_ref[pl.ds(plane + base, plan.erode_block), tiles])
            for n in range(plan.erode_block):
                at = plane + n + base
                cur = pull_ref[at, tiles]

                def load(offset, at=at):
                    return pull_ref[at, 8 + offset : 8 + offset + plan.tiles]

                total = cur + pull_ref[at - 1, tiles] + pull_ref[at + 1, tiles]
                total = total + x_neighbours(plan, mask, load, cur)
                total = total + beside[n] + wt_ref[at]
                if not ending:
                    total = total * cross_ref[kind_of(plan, rank, plane + n)[0]]
                next_ref[at, tiles] = total

        over(-reach, zc + 2 * reach, plan.erode_block, join)

    def pair(n, carry):
        section(2 * n, 0, 1, False)
        section(2 * n + 1, 1, 0, False)
        return carry

    lax.fori_loop(0, ITERS // 2, pair, 0)
    section(ITERS, 0, 1, True)
    mine_ref[...] = pull1_ref[base - 1 : base + zc + 1, tiles]
    for h in range(1, hops + 1):
        n = plan.back_count(h)
        first = base + h * zc - 1
        up[h - 1][...] = pull1_ref[first : first + n, tiles]
        first = base + (1 - h) * zc - n + 1
        down[h - 1][...] = pull1_ref[first : first + n, tiles]


def finish_kernel(plan, *refs):
    hops = plan.back_hops
    pos_ref, sums_ref, skel_ref, p_ref, target_ref, ts_ref, mine_ref = refs[:7]
    below, above = refs[7 : 7 + hops], refs[7 + hops : 7 + 2 * hops]
    out_ref, loss_ref, bias_ref, h_ref, grad_ref = refs[7 + 2 * hops :]
    rank = pos_ref[0]
    zc = plan.zc
    s1, s2, s5, s6, s7 = get_sums(sums_ref, 5)
    s3, s4 = get_sums(skel_ref, 2)
    prec = (s1 + 1.0) / (s2 + 1.0)
    sens = (s3 + 1.0) / (s4 + 1.0)
    both = prec + sens
    volume = s6 + s7 + 1.0
    cl_loss = 1.0 - 2.0 * prec * sens / both
    dice_loss = 1.0 - (2.0 * s5 + 1.0) / volume
    loss_ref[...] = jnp.broadcast_to(0.5 * dice_loss + 0.5 * cl_loss, (8, LANES))
    l0 = -(sens / both) * (sens / both) / (s2 + 1.0)
    l2 = -(prec / both) * (prec / both) / (s4 + 1.0)
    l4 = -1.0 / volume
    l5 = 0.5 * (2.0 * s5 + 1.0) / (volume * volume)

    h_ref[...] = mine_ref[...]
    for h in range(1, hops + 1):
        n = plan.back_count(h)
        h_ref[:n] += below[h - 1][...]
        h_ref[plan.span - n :] += above[h - 1][...]

    total = jnp.zeros((plan.tiles, LANES), f32)
    for n in range(plan.span):
        inside = 1.0 - kind_of(plan, rank, n - 1)[1]
        predict = p_ref[n]
        skel = l0 * jnp.exp(-temper * predict) * h_ref[n]
        whole = skel + l2 * ts_ref[n] + l4 * target_ref[n] + l5
        grad = whole * predict * (1.0 - predict) * inside
        grad_ref[n * plan.tiles : (n + 1) * plan.tiles] = grad
        if 1 <= n <= zc:
            total = total + grad
    bias_ref[...] = jnp.sum(total.reshape(-1, 8, LANES), axis=0)
    lane = lane_iota((1, LANES))

    def column(tile):
        return [
            grad_ref[pl.ds(plan.tiles + tile, zc, stride=plan.tiles)],
            grad_ref[tile : tile + 1],
            grad_ref[(zc + 1) * plan.tiles + tile : (zc + 1) * plan.tiles + tile + 1],
        ]

    for a in range(plan.gx):
        pieces = [column(a * plan.own + q) for q in range(plan.own)]
        zero = [jnp.zeros((zc, LANES), f32)] + [jnp.zeros((1, LANES), f32)] * 2
        after = column((a + 1) * plan.own) if a < plan.gx - 1 else zero
        before = column(a * plan.own - 1) if a > 0 else zero
        if plan.shared:
            pieces.append(
                [
                    jnp.where(lane < plan.Y, x, 0.0) + jnp.where(lane >= LANES - plan.Y, y, 0.0)
                    for x, y in zip(after, before)
                ]
            )
        else:
            pieces += [after, before]
        edges = [edge for piece in pieces for edge in piece[1:]]
        rows = plan.R16
        edges += [jnp.zeros((1, LANES), f32)] * (plan.extra16 * rows - len(edges))
        whole = [piece[0] for piece in pieces]
        if rows > zc:
            fill = jnp.zeros((rows - zc, LANES), f32)
            whole = [jnp.concatenate([piece, fill], axis=0) for piece in whole]
        whole += [
            jnp.concatenate(edges[n * rows : (n + 1) * rows], axis=0) for n in range(plan.extra16)
        ]
        for q, piece in enumerate(whole):
            piece = piece.astype(bf16)
            for b in range(plan.gy):
                out_ref[a * plan.gy + b, q] = piece


def weight_kernel(
    plan, pos_ref, far_ref, bias_ref, got_ref, gw_ref, g_ref, dw_ref, f_ref, sem_ref
):
    copies = stream(plan, far_ref, f_ref, sem_ref)
    rows, inner = plan.Y, plan.ch * plan.ny
    zc, nz = plan.zc, plan.nz
    lane = lane_iota((rows, nz))
    places = {}
    for x in range(-1, plan.nx + 1):
        tile, first = plan.slot(x)
        places.setdefault(tile, {})[first] = x
    for tile in range(plan.sent):
        order = [plan.member_now(j, pos_ref) for j in range(plan.members)]
        stack = [got_ref[p, tile].astype(f32)[:zc] for p in order]
        turned = jnp.concatenate(stack, axis=0).T
        ends = []
        for end, p in ((0, order[0]), (1, order[-1])):
            n = 2 * tile + end
            row = got_ref[p, plan.sent + n // plan.R16].astype(f32)
            ends.append(row[n % plan.R16 : n % plan.R16 + 1])
        ends = jnp.concatenate(ends + [jnp.zeros((LANES - 2, LANES), f32)], axis=0).T
        for first, x in places[tile].items():
            g = turned[first : first + rows]
            end = ends[first : first + rows]
            down = jnp.where(lane == nz - 1, pltpu.roll(end, nz - 2, 1), pltpu.roll(g, nz - 1, 1))
            up = jnp.where(lane == 0, end, pltpu.roll(g, 1, 1))
            g_ref[x + 1] = jnp.concatenate([down, g, up], axis=0).astype(bf16)

    dw_ref[...] = jnp.zeros_like(dw_ref)

    width = plan.nx // PARTS
    for n in range(PARTS):
        copies[n].wait()
        dw_ref[...] += lax.dot_general(
            moved_columns(g_ref, n * width, width),
            columns(plan, f_ref, n * width, width),
            (((1,), (1,)), ((), ())),
            preferred_element_type=f32,
        )

    tap_y = tap_condition(plan, pos_ref[1], (rows, inner), 0, 1)
    taps = []
    for t in range(27):
        i, j, k = t // 9, t // 3 % 3, t % 3
        at = (3 * i + k) * rows
        taps.append(jnp.sum(jnp.where(tap_y == j, dw_ref[at : at + rows], 0.0), axis=0, keepdims=True))
    taps += [jnp.zeros((1, inner), f32)] * 5
    taps = jnp.concatenate(taps, axis=0)
    high = taps.astype(bf16)
    taps = taps - high.astype(f32)
    middle = taps.astype(bf16)
    low = (taps - middle.astype(f32)).astype(bf16)
    place = (
        lax.broadcasted_iota(jnp.int32, (inner, LANES), 0) // plan.ny
        == lax.broadcasted_iota(jnp.int32, (inner, LANES), 1)
    )
    sums = jnp.dot(
        jnp.concatenate([high, middle, low], axis=0),
        place.astype(f32).astype(bf16),
        preferred_element_type=f32,
    )
    sums = sums[0:32] + sums[32:64] + sums[64:96]
    total = sums[0:8]
    for n in range(1, 4):
        total = total + pltpu.roll(sums[8 * n : 8 * n + 8], 32 * n, 1)
    spot = (row_iota((8, LANES)) == 3) & (lane_iota((8, LANES)) == 96)
    total = jnp.where(spot, jnp.sum(bias_ref[...]), total)
    gw_ref[...] = jnp.broadcast_to(total[None], (plan.ranks, 8, LANES))


def wide_kernel(plan, pos_ref, wt_ref, after_ref, wide_ref):
    del after_ref
    rows, inner, bands = plan.Y, plan.ch * plan.ny, 9 * plan.Y
    spread = (
        lax.broadcasted_iota(jnp.int32, (inner, plan.ch), 0) // plan.ny
        == lax.broadcasted_iota(jnp.int32, (inner, plan.ch), 1)
    )
    spread = spread.astype(f32).astype(bf16)
    tap_y = tap_condition(plan, pos_ref[1], (inner, bands), 1, 0)
    wide = jnp.zeros((inner, bands), f32)
    tap = lax.broadcasted_iota(jnp.int32, (27, bands), 0)
    band = lax.broadcasted_iota(jnp.int32, (27, bands), 1) // rows
    for j in range(3):
        pick = (tap == 9 * (band // 3) + 3 * j + band % 3).astype(f32).astype(bf16)
        chosen = jnp.dot(wt_ref[...], pick, preferred_element_type=f32).astype(bf16)
        full = jnp.dot(spread, chosen, preferred_element_type=f32)
        wide = jnp.where(tap_y == j, full, wide)
    wide_ref[...] = wide.astype(bf16)


def feature_kernel(plan, wide_ref, g_ref, after_ref, gf_ref):
    del after_ref
    width = plan.nx // PARTS
    for n in range(PARTS):
        out = jnp.dot(
            wide_ref[...],
            moved_columns(g_ref, n * width, width),
            preferred_element_type=f32,
        )
        for x in range(width):
            part = out[:, x * plan.nz : (x + 1) * plan.nz].astype(bf16)
            gf_ref[:, n * width + x] = part.reshape(plan.ch, plan.ny, plan.nz)


def final_kernel(plan, got_ref, gw_ref, gb_ref):
    total = jnp.sum(got_ref[...], axis=0)
    for n in range(4):
        count = min(8, 27 - 8 * n)
        gw_ref[8 * n : 8 * n + count] = total[:count, 32 * n : 32 * n + plan.ch]
    gb_ref[...] = total[3:4, 96:97]


VMEM = pl.BlockSpec(memory_space=pltpu.VMEM)
SMEM = pl.BlockSpec(memory_space=pltpu.SMEM)
ANY = pl.BlockSpec(memory_space=pl.ANY)
FAR = pl.BlockSpec(memory_space=pltpu.HBM)
MIB = 1024 * 1024


def shape(dims, dtype=f32):
    return jax.ShapeDtypeStruct(dims, dtype)


def held(dims, dtype):
    if len(dims) < 2:
        return 4096
    size = jnp.dtype(dtype).itemsize
    rows = 8 * 4 // size
    total = -(-dims[-2] // rows) * rows * -(-dims[-1] // LANES) * LANES * size
    for n in dims[:-2]:
        total *= n
    return total


def limits(arrays, scratch, micros):
    total = sum(held(a.shape, a.dtype) for a in arrays)
    total += sum(held(a.shape, a.dtype) for a in scratch if len(a.shape) > 1)
    limit = min(63 * MIB, total + total // 8 + 4 * MIB)
    return dict(
        compiler_params=pltpu.CompilerParams(vmem_limit_bytes=limit),
        cost_estimate=pl.CostEstimate(
            flops=0, transcendentals=0, bytes_accessed=int(micros * 2.5e4)
        ),
    )


def per_device(mesh_shape, features, weight, bias, label):
    plan = Plan(mesh_shape, features.shape)
    members, sent, tiles = plan.members, plan.sent, plan.tiles
    inner, bands = plan.ch * plan.ny, 9 * plan.Y
    x, y, z = (lax.axis_index(axis).astype(jnp.int32) for axis in ALL_AXES)
    mine = y * plan.gx + jnp.where(y % 2 == 0, x, plan.gx - 1 - x)
    place = z * members + jnp.where(z % 2 == 0, mine, members - 1 - mine)
    pos = jnp.stack([place, y])

    def call(
        kernel, out_shape, in_specs, operands, micros, scratch=(), out_specs=None
    ):
        outs = jax.tree.leaves(out_shape)
        ins = [a for spec, a in zip(in_specs, operands) if spec is VMEM]
        return pl.pallas_call(
            functools.partial(kernel, plan),
            out_shape=out_shape,
            in_specs=in_specs,
            out_specs=out_specs or jax.tree.map(lambda s: VMEM, out_shape),
            scratch_shapes=list(scratch),
            **limits(ins + outs, scratch, micros),
        )(*operands)

    def exchange(array):
        return lax.all_to_all(array, GROUP, 0, 0, tiled=True)

    def everywhere(array):
        return lax.all_to_all(array, ALL_AXES, 0, 0, tiled=True)

    def hop(array, distance):
        def device(r):
            z = r // members
            return plan.member(r % members, z % 2 == 1) * plan.gz + z

        pairs = [
            (device(r), device(r + distance))
            for r in range(plan.ranks)
            if 0 <= r + distance < plan.ranks
        ]
        return lax.ppermute(array, ALL_AXES, pairs)

    turned = weight.T
    features, weight, label = (
        pltpu.with_memory_space_constraint(a, pltpu.HBM) for a in (features, weight, label)
    )
    features_near = [pltpu.VMEM(features.shape, bf16), pltpu.SemaphoreType.DMA((PARTS,))]
    sent_logits = call(
        conv_kernel,
        shape((members, sent + plan.extra, plan.R, LANES)),
        [SMEM, VMEM, FAR, VMEM],
        (pos, weight, features, label),
        7,
        [
            pltpu.VMEM((bands, inner), bf16),
            pltpu.VMEM((plan.nx + 2, 3 * plan.Y, plan.nz), f32),
        ]
        + features_near,
    )

    def planes(array):
        return array.reshape(-1, tiles, LANES)

    zc, rest = plan.zc, plan.rest
    short = shape(((rest + 1 + -(-rest // 2)) * tiles, LANES))
    whole, label_own, head, tail = call(
        gather_kernel,
        [
            shape(((zc + 2 + -(-zc // 2)) * tiles, LANES)),
            shape((zc * tiles, LANES)),
            short,
            short,
        ],
        [VMEM],
        (exchange(sent_logits),),
        1.5,
    )
    whole, label_own, head, tail = (planes(part) for part in (whole, label_own, head, tail))
    around = [
        hop(whole if h < plan.hops else part, sign * h)
        for sign, part in ((1, tail), (-1, head))
        for h in range(1, plan.hops + 1)
    ]

    slab = (zc, tiles, LANES)
    span = (plan.span, tiles, LANES)
    everyone = shape((plan.ranks, 8, LANES))
    table = pltpu.VMEM((3, tiles, LANES), f32)

    records = pltpu.HBM((SECTIONS, plan.records, tiles, LANES), f32)
    y_near = pltpu.VMEM((2 * LANES, LANES), bf16)
    record_near = [
        y_near,
        pltpu.VMEM(records.shape, f32),
        pltpu.SemaphoreType.DMA((SECTIONS,)),
    ]
    record, predict, sums = call(
        forward_kernel,
        [records, shape(span), everyone],
        [SMEM, SMEM] + [VMEM] * (2 + 2 * plan.hops),
        (pos, bias, label_own, whole, *around),
        11,
        [
            pltpu.VMEM((plan.planes, plan.pad, LANES), f32),
            pltpu.VMEM((plan.planes, plan.pad, LANES), f32),
            pltpu.VMEM((plan.planes, tiles, LANES), f32),
            pltpu.VMEM((plan.planes, tiles, LANES), f32),
            pltpu.VMEM((zc, plan.pad, LANES), f32),
            pltpu.VMEM(slab, f32),
            table,
            table,
        ]
        + record_near,
        [FAR, VMEM, VMEM],
    )
    record = pltpu.with_memory_space_constraint(record, pltpu.HBM)
    sums = everywhere(sums)
    room = plan.win + 2 + plan.erode_block
    target, ts, skel_sums = call(
        target_kernel,
        [shape(span), shape(span), everyone],
        [SMEM] + [VMEM] * (2 + 2 * plan.hops),
        (pos, predict, label_own, *around),
        13,
        [
            pltpu.VMEM((plan.win, tiles, LANES), f32),
            pltpu.VMEM((room, plan.pad, LANES), f32),
            pltpu.VMEM((room, plan.pad, LANES), f32),
            pltpu.VMEM((room, tiles, LANES), f32),
            pltpu.VMEM((plan.span, plan.pad, LANES), f32),
            table,
            table,
            y_near,
        ],
    )
    skel_sums = everywhere(skel_sums)
    outer = [
        shape((plan.back_count(h), tiles, LANES)) for h in range(1, plan.back_hops + 1)
    ]
    mine, *outer = call(
        backward_kernel,
        [shape(span)] + outer * 2,
        [SMEM, VMEM, VMEM, FAR],
        (pos, sums, label_own, record),
        11,
        [
            pltpu.VMEM(slab, f32),
            pltpu.VMEM((zc + 4, tiles, LANES), f32),
            pltpu.VMEM((plan.pull_planes, tiles, LANES), f32),
            pltpu.VMEM((plan.span, plan.pad, LANES), f32),
            pltpu.VMEM((plan.pull_planes, plan.pad, LANES), f32),
            pltpu.VMEM((plan.pull_planes, plan.pad, LANES), f32),
            table,
        ]
        + record_near,
    )
    wide = call(
        wide_kernel, shape((inner, bands), bf16), [SMEM, VMEM, ANY], (pos, turned, mine), 2
    )
    beyond = []
    for sign, arrays in ((1, outer[: plan.back_hops]), (-1, outer[plan.back_hops :])):
        for h in range(1, plan.back_hops + 1):
            beyond.append(hop(arrays[h - 1], sign * h))
    grad_sent, loss, bias_part = call(
        finish_kernel,
        [
            shape((members, sent + plan.extra16, plan.R16, LANES), bf16),
            shape((8, LANES)),
            shape((8, LANES)),
        ],
        [SMEM] + [VMEM] * (6 + 2 * plan.back_hops),
        (pos, sums, skel_sums, predict, target, ts, mine, *beyond),
        2,
        [pltpu.VMEM(span, f32), pltpu.VMEM((plan.span * tiles, LANES), f32)],
    )

    moved = shape((plan.nx + 2, 3 * plan.Y, plan.nz), bf16)
    partial, g = call(
        weight_kernel,
        [shape((plan.ranks, 8, LANES)), moved],
        [SMEM, FAR, VMEM, VMEM],
        (pos, features, bias_part, exchange(grad_sent)),
        5,
        [pltpu.VMEM((bands, inner), f32)] + features_near,
    )
    grad_features = call(
        feature_kernel,
        shape(features.shape, bf16),
        [VMEM, VMEM, ANY],
        (wide, g, partial),
        5,
    )
    grad_weight, grad_bias = call(
        final_kernel,
        [shape((27, plan.ch)), shape((1, 1))],
        [VMEM],
        (everywhere(partial),),
        1.5,
    )
    return (loss[0, :1], grad_features, grad_weight, grad_bias.reshape(1))


def solution(mesh):
    in_specs = (P(None, "gx", "gy", "gz"), P(), P(), P("gx", "gy", "gz"))
    out_specs = (P(), P(None, "gx", "gy", "gz"), P(), P())

    def body(*args):
        return per_device(dict(mesh.shape), *args)

    return jax.shard_map(
        body, mesh=mesh, in_specs=in_specs, out_specs=out_specs, check_vma=False
    )
```

profile of v0, /device:TPU:0, one launch (start us, length us, event | category | flops | bytes accessed | tf_op | source)
XLA Modules:
  0.0 109.7 jit_solution(2381182513387098764)
XLA Ops:
  0.7 0.1 pad_add_fusion.pos_ref.refs_0_
  0.7 3.6 %shard_map.75 = f32[8,6,16,128]{3,2,1,0:T(8,128)S(1)} custom-call(s32[2]{0:T(128)S(1)} %pad_add_fusion.pos_ref.refs_0_, bf16[27,32]{1,0:T(8,128)(2,1)} %w_ref.1, bf16[32,16,16,128]{3,2,1,0:T(8,128)(2,1)} %far_ref.3, s32[16,16,128]{2,1,0:T(8,128)} %label_ref.1), custom_call_target="tpu_custom_call" | custom-call | bytes 175000 | tf_op jit(solution)/shard_map/pallas_call | solution.py:957
  4.3 12.8 %all_to_all.25.got_ref = f32[8,6,16,128]{3,2,1,0:T(8,128)S(1)} all-to-all(f32[8,6,16,128]{3,2,1,0:T(8,128)S(1)} %shard_map.75), channel_id=1, replica_groups=mesh['gx'=4,'gy'=2,'gz'=4] {'gx','gy'}, dimensions={0} | all-to-all | bytes 786432 | tf_op jit(solution)/shard_map/all_to_all | solution.py:967
  17.1 0.2 shard_map.76
  17.3 2.1 %collective-permute-start = (f32[21,16,128]{2,1,0:T(8,128)S(1)}, f32[21,16,128]{2,1,0:T(8,128)S(1)}, u32[]{:S(2)}, u32[]{:S(2)}) collective-permute-start(f32[21,16,128]{2,1,0:T(8,128)S(1)} %bitcast.15), channel_id=1, source_target_pairs={{0,8},{8,16},{16,24},{24,28},{28,20},{20,12},{12,4},{4,5},{5,13},{... | collective-permute-start | bytes 516104 | tf_op jit(solution)/shard_map/ppermute | solution.py:982
  19.4 1.3 %collective-permute-start.1 = (f32[21,16,128]{2,1,0:T(8,128)S(1)}, f32[21,16,128]{2,1,0:T(8,128)S(1)}, u32[]{:S(2)}, u32[]{:S(2)}) collective-permute-start(f32[21,16,128]{2,1,0:T(8,128)S(1)} %bitcast.14), channel_id=1, source_target_pairs={{8,0},{16,8},{24,16},{28,24},{20,28},{12,20},{4,12},{5,4},{13,5},{... | collective-permute-start | bytes 516104 | tf_op jit(solution)/shard_map/ppermute | solution.py:982
  21.4 0.0 collective-permute-done.refs_4_.refs_3_
  21.4 1.5 %collective-permute-done.1.refs_5_.refs_4_ = f32[21,16,128]{2,1,0:T(8,128)S(1)} collective-permute-done((f32[21,16,128]{2,1,0:T(8,128)S(1)}, f32[21,16,128]{2,1,0:T(8,128)S(1)}, u32[]{:S(2)}, u32[]{:S(2)}) %collective-permute-start.1) | collective-permute-done | bytes 172064 | tf_op jit(solution)/shard_map/ppermute | solution.py:982
  22.9 13.2 %shard_map.77 = (f32[11,66,16,128]{3,2,1,0:T(8,128)}, f32[18,16,128]{2,1,0:T(8,128)S(1)}, f32[32,8,128]{2,1,0:T(8,128)}) custom-call(s32[2]{0:T(128)S(1)} %pad_add_fusion.pos_ref.refs_0_, f32[1]{0:T(128)S(6)} %copy.9.refs_1_, f32[16,16,128]{2,1,0:T(8,128)S(1)} %bitcast.9, f32[26,16,128]{2,1,0:T(8,128)S(1)} %bitcast.12, ...), custom_call_target="tpu_custom_call" | custom-call | bytes 275000 | tf_op jit(solution)/shard_map/pallas_call | solution.py:957
  36.1 8.7 %all-to-all-start.1 = ((f32[32,8,128]{2,1,0:T(8,128)}), f32[32,8,128]{2,1,0:T(8,128)S(1)}, u32[]{:S(2)}, u32[]{:S(2)}) async-start(f32[32,8,128]{2,1,0:T(8,128)} %get-tuple-element.28), calls=%async_computation.1 | async-start | bytes 262144 | tf_op jit(solution)/shard_map/all_to_all | solution.py:970
  44.9 12.3 %shard_map.78 = (f32[18,16,128]{2,1,0:T(8,128)S(1)}, f32[18,16,128]{2,1,0:T(8,128)S(1)}, f32[32,8,128]{2,1,0:T(8,128)}) custom-call(s32[2]{0:T(128)S(1)} %pad_add_fusion.pos_ref.refs_0_, f32[18,16,128]{2,1,0:T(8,128)S(1)} %get-tuple-element.29.refs_1_.refs_3_, f32[16,16,128]{2,1,0:T(8,128)S(1)} %bitcast.10, ...), custom_call_target="tpu_custom_call" | custom-call | bytes 325000 | tf_op jit(solution)/shard_map/pallas_call | solution.py:957
  57.1 0.0 all-to-all-done.1.refs_1_
  57.1 5.8 %all-to-all-start.2 = ((f32[32,8,128]{2,1,0:T(8,128)}), f32[32,8,128]{2,1,0:T(8,128)S(1)}, u32[]{:S(2)}, u32[]{:S(2)}) async-start(f32[32,8,128]{2,1,0:T(8,128)} %get-tuple-element.30), calls=%async_computation.2 | async-start | bytes 262144 | tf_op jit(solution)/shard_map/all_to_all | solution.py:970
  63.0 11.4 %shard_map.79 = (f32[18,16,128]{2,1,0:T(8,128)S(1)}, f32[13,16,128]{2,1,0:T(8,128)S(1)}, f32[13,16,128]{2,1,0:T(8,128)S(1)}) custom-call(s32[2]{0:T(128)S(1)} %pad_add_fusion.pos_ref.refs_0_, f32[32,8,128]{2,1,0:T(8,128)S(1)} %all-to-all-done.1.refs_1_, f32[16,16,128]{2,1,0:T(8,128)S(1)} %bitcast.11, f32[11,66,16,128]{3,2,1,0:T(8,128)} %get-tuple-element.33.refs_3_), custom_call_target="tpu_custom_call" | custom-call | bytes 275000 | tf_op jit(solution)/shard_map/pallas_call | solution.py:957
  74.4 0.0 copy-start
  74.4 2.2 %collective-permute-start.2 = (f32[13,16,128]{2,1,0:T(8,128)S(1)}, f32[13,16,128]{2,1,0:T(8,128)S(1)}, u32[]{:S(2)}, u32[]{:S(2)}) collective-permute-start(f32[13,16,128]{2,1,0:T(8,128)S(1)} %get-tuple-element.35), channel_id=1, source_target_pairs={{0,8},{8,16},{16,24},{24,28},{28,20},{20,12},{12,4},{4,5},{5,13},{... | collective-permute-start | bytes 319496 | tf_op jit(solution)/shard_map/ppermute | solution.py:982
  76.6 1.3 %collective-permute-start.3 = (f32[13,16,128]{2,1,0:T(8,128)S(1)}, f32[13,16,128]{2,1,0:T(8,128)S(1)}, u32[]{:S(2)}, u32[]{:S(2)}) collective-permute-start(f32[13,16,128]{2,1,0:T(8,128)S(1)} %get-tuple-element.36), channel_id=1, source_target_pairs={{8,0},{16,8},{24,16},{28,24},{20,28},{12,20},{4,12},{5,4},{13,5},{... | collective-permute-start | bytes 319496 | tf_op jit(solution)/shard_map/ppermute | solution.py:982
  77.9 0.0 all-to-all-done.2.refs_2_
  77.9 0.0 collective-permute-done.2.refs_7_
  77.9 3.0 %collective-permute-done.3.refs_8_ = f32[13,16,128]{2,1,0:T(8,128)S(1)} collective-permute-done((f32[13,16,128]{2,1,0:T(8,128)S(1)}, f32[13,16,128]{2,1,0:T(8,128)S(1)}, u32[]{:S(2)}, u32[]{:S(2)}) %collective-permute-start.3) | collective-permute-done | bytes 106528 | tf_op jit(solution)/shard_map/ppermute | solution.py:982
  81.0 0.8 shard_map.80
  81.8 11.6 %all_to_all.26.got_ref = bf16[8,6,16,128]{3,2,1,0:T(8,128)(2,1)S(1)} all-to-all(bf16[8,6,16,128]{3,2,1,0:T(8,128)(2,1)S(1)} %get-tuple-element.39), channel_id=1, replica_groups=mesh['gx'=4,'gy'=2,'gz'=4] {'gx','gy'}, dimensions={0} | all-to-all | bytes 393216 | tf_op jit(solution)/shard_map/all_to_all | solution.py:967
  93.4 4.0 %shard_map.82 = (f32[32,8,128]{2,1,0:T(8,128)}, bf16[18,96,128]{2,1,0:T(8,128)(2,1)S(1)}) custom-call(s32[2]{0:T(128)S(1)} %pad_add_fusion.pos_ref.refs_0_, bf16[32,16,16,128]{3,2,1,0:T(8,128)(2,1)} %far_ref.3, f32[8,128]{1,0:T(8,128)S(1)} %get-tuple-element.38.bias_ref, bf16[8,6,16,128]{3,2,1,0:T(8,128)(2,1)S(1)} %all_to_all.26.got_ref), custom_call_target="tpu_custom_call" | custom-call | bytes 125000 | tf_op jit(solution)/shard_map/pallas_call | solution.py:957
  97.4 3.8 %all-to-all-start.4 = ((f32[32,8,128]{2,1,0:T(8,128)}), f32[32,8,128]{2,1,0:T(8,128)S(1)}, u32[]{:S(2)}, u32[]{:S(2)}) async-start(f32[32,8,128]{2,1,0:T(8,128)} %get-tuple-element.41.after_ref), calls=%async_computation.4 | async-start | bytes 262144 | tf_op jit(solution)/shard_map/all_to_all | solution.py:970
  101.2 0.0 copy-done
  101.2 0.1 copy.8
  101.3 1.4 %shard_map.81.wide_ref = bf16[512,288]{1,0:T(8,128)(2,1)S(1)} custom-call(s32[2]{0:T(128)S(1)} %pad_add_fusion.pos_ref.refs_0_, bf16[32,27]{1,0:T(8,128)(2,1)S(1)} %bitcast.13, f32[18,16,128]{2,1,0:T(8,128)S(1)} %get-tuple-element.34.refs_6_.after_ref), custom_call_target="tpu_custom_call" | custom-call | bytes 50000 | tf_op jit(solution)/shard_map/pallas_call | solution.py:957
  102.7 0.5 slice.3
  103.2 2.6 %shard_map.83 = bf16[32,16,16,128]{3,2,1,0:T(8,128)(2,1)} custom-call(bf16[512,288]{1,0:T(8,128)(2,1)S(1)} %shard_map.81.wide_ref, bf16[18,96,128]{2,1,0:T(8,128)(2,1)S(1)} %get-tuple-element.40.g_ref, f32[32,8,128]{2,1,0:T(8,128)} %get-tuple-element.41.after_ref), custom_call_target="tpu_custom_call" | custom-call | bytes 125000 | tf_op jit(solution)/shard_map/pallas_call | solution.py:957
  105.8 3.2 %all-to-all-done.4.got_ref = f32[32,8,128]{2,1,0:T(8,128)S(1)} async-done(((f32[32,8,128]{2,1,0:T(8,128)}), f32[32,8,128]{2,1,0:T(8,128)S(1)}, u32[]{:S(2)}, u32[]{:S(2)}) %all-to-all-start.4) | async-done | bytes 131104 | tf_op jit(solution)/shard_map/all_to_all | solution.py:970
  109.0 0.7 shard_map.84
Async XLA Ops:
  17.3 4.0 %collective-permute-start = (f32[21,16,128]{2,1,0:T(8,128)S(1)}, f32[21,16,128]{2,1,0:T(8,128)S(1)}, u32[]{:S(2)}, u32[]{:S(2)}) collective-permute-start(f32[21,16,128]{2,1,0:T(8,128)S(1)} %bitcast.15), channel_id=1, source_target_pairs={{0,8},{8,16},{16,24},{24,28},{28,20},{20,12},{12,4},{4,5},{5,13},{... | collective-permute-start | bytes 516104 | tf_op jit(solution)/shard_map/ppermute | solution.py:982
  19.4 3.5 %collective-permute-start.1 = (f32[21,16,128]{2,1,0:T(8,128)S(1)}, f32[21,16,128]{2,1,0:T(8,128)S(1)}, u32[]{:S(2)}, u32[]{:S(2)}) collective-permute-start(f32[21,16,128]{2,1,0:T(8,128)S(1)} %bitcast.14), channel_id=1, source_target_pairs={{8,0},{16,8},{24,16},{28,24},{20,28},{12,20},{4,12},{5,4},{13,5},{... | collective-permute-start | bytes 516104 | tf_op jit(solution)/shard_map/ppermute | solution.py:982
  36.1 21.0 %all-to-all-start.1 = ((f32[32,8,128]{2,1,0:T(8,128)}), f32[32,8,128]{2,1,0:T(8,128)S(1)}, u32[]{:S(2)}, u32[]{:S(2)}) async-start(f32[32,8,128]{2,1,0:T(8,128)} %get-tuple-element.28), calls=%async_computation.1 | async-start | bytes 262144 | tf_op jit(solution)/shard_map/all_to_all | solution.py:970
  57.1 20.8 %all-to-all-start.2 = ((f32[32,8,128]{2,1,0:T(8,128)}), f32[32,8,128]{2,1,0:T(8,128)S(1)}, u32[]{:S(2)}, u32[]{:S(2)}) async-start(f32[32,8,128]{2,1,0:T(8,128)} %get-tuple-element.30), calls=%async_computation.2 | async-start | bytes 262144 | tf_op jit(solution)/shard_map/all_to_all | solution.py:970
  74.4 26.8 %copy-start = (bf16[27,32]{1,0:T(8,128)(2,1)S(1)}, bf16[27,32]{1,0:T(8,128)(2,1)}, u32[]{:S(2)}) copy-start(bf16[27,32]{1,0:T(8,128)(2,1)} %w_ref.1) | copy-start | bytes 5188
  74.4 3.5 %collective-permute-start.2 = (f32[13,16,128]{2,1,0:T(8,128)S(1)}, f32[13,16,128]{2,1,0:T(8,128)S(1)}, u32[]{:S(2)}, u32[]{:S(2)}) collective-permute-start(f32[13,16,128]{2,1,0:T(8,128)S(1)} %get-tuple-element.35), channel_id=1, source_target_pairs={{0,8},{8,16},{16,24},{24,28},{28,20},{20,12},{12,4},{4,5},{5,13},{... | collective-permute-start | bytes 319496 | tf_op jit(solution)/shard_map/ppermute | solution.py:982
  76.6 4.3 %collective-permute-start.3 = (f32[13,16,128]{2,1,0:T(8,128)S(1)}, f32[13,16,128]{2,1,0:T(8,128)S(1)}, u32[]{:S(2)}, u32[]{:S(2)}) collective-permute-start(f32[13,16,128]{2,1,0:T(8,128)S(1)} %get-tuple-element.36), channel_id=1, source_target_pairs={{8,0},{16,8},{24,16},{28,24},{20,28},{12,20},{4,12},{5,4},{13,5},{... | collective-permute-start | bytes 319496 | tf_op jit(solution)/shard_map/ppermute | solution.py:982
  97.4 11.6 %all-to-all-start.4 = ((f32[32,8,128]{2,1,0:T(8,128)}), f32[32,8,128]{2,1,0:T(8,128)S(1)}, u32[]{:S(2)}, u32[]{:S(2)}) async-start(f32[32,8,128]{2,1,0:T(8,128)} %get-tuple-element.41.after_ref), calls=%async_computation.4 | async-start | bytes 262144 | tf_op jit(solution)/shard_map/all_to_all | solution.py:970
where the time goes:
time: 110 us
  Pallas kernels  50.3 us (46%)
  starting transfers between devices  25.1 us (23%)
  blocking collectives  24.4 us (22%)
  waiting for transfers between devices  7.71 us (7%)
  between operations  1.45 us (1%)
    pallas_call x10, Pallas kernels, call(): pl.pallas_call(functools.partial(kernel, plan), out_shape=out_shape, in_s...  50.3 us
    all_to_all x2, blocking collectives, exchange(): return lax.all_to_all(array, GROUP, 0, 0, tiled=True)  24.4 us
    all_to_all x3, starting transfers between devices, everywhere(): return lax.all_to_all(array, ALL_AXES, 0, 0, tiled=True)  18.3 us
    ppermute x4, starting transfers between devices, hop(): return lax.ppermute(array, ALL_AXES, pairs)  6.83 us
    ppermute x4, waiting for transfers between devices, hop(): return lax.ppermute(array, ALL_AXES, pairs)  4.55 us
    all_to_all x3, waiting for transfers between devices, everywhere(): return lax.all_to_all(array, ALL_AXES, 0, 0, tiled=True)  3.17 us
  transfers between devices with their start and end apart: 7, of which 3 were waited for; matrix products, arithmetic and copies ran while one was open for 1% of the time, Pallas kernels for 25%

commit v1 on v0

--- a/solution.py
+++ b/solution.py
@@ -107,17 +107,28 @@
     return lax.broadcasted_iota(jnp.int32, shape, len(shape) - 2)
 
 
-def masks(plan):
-    return lane_iota((plan.tiles, LANES))
-
-
-def x_neighbours(plan, mask, load, cur):
-    lower, upper = load(-1), load(1)
-    if plan.Y == LANES:
-        return lower + upper
-    lower = pltpu.roll(jnp.where(mask >= LANES - plan.Y, lower, cur), plan.Y, 1)
-    upper = pltpu.roll(jnp.where(mask < plan.Y, upper, cur), LANES - plan.Y, 1)
-    return lower + upper
+def place_of(plan, x):
+    return x % plan.tiles, x // plan.tiles
+
+
+def in_group(plan, group):
+    return lane_iota((1, LANES)) // plan.Y == group
+
+
+def x_neighbours(plan, ref, at):
+    return ref[at, 7 : 7 + plan.tiles] + ref[at, 9 : 9 + plan.tiles]
+
+
+def wrap(plan, ref, at, value):
+    tiles = plan.tiles
+    ref[at, 8 : 8 + tiles] = value
+    if plan.per == 1:
+        return
+    lane = lane_iota((8, LANES))
+    lower = pltpu.roll(value[tiles - 8 :], plan.Y, 1)
+    upper = pltpu.roll(value[:8], LANES - plan.Y, 1)
+    ref[at, 7:8] = jnp.where(lane < plan.Y, 0.0, lower)[7:8]
+    ref[at, 8 + tiles : 9 + tiles] = jnp.where(lane >= LANES - plan.Y, 0.0, upper)[0:1]
 
 
 def y_matrix(plan, ref):
@@ -136,8 +147,8 @@
 
 
 def count_tables(plan, cross_ref, box_ref):
-    flat = row_iota((plan.tiles, LANES)) * LANES + lane_iota((plan.tiles, LANES))
-    y, x = flat % plan.Y, flat // plan.Y
+    lane = lane_iota((plan.tiles, LANES))
+    y, x = lane % plan.Y, lane // plan.Y * plan.tiles + row_iota((plan.tiles, LANES))
 
     def along(spot, size):
         return 3.0 - (spot == 0).astype(f32) - (spot == size - 1).astype(f32)
@@ -301,34 +312,52 @@
             values.append(got_ref[p, at, n % plan.R : n % plan.R + 1])
         return values
 
+    parts = {t: [] for t in range(tiles)}
+    labels = {t: jnp.zeros((zc, LANES), f32) for t in range(tiles)}
+
+    def move(value, group, to):
+        shift = (to - group) * plan.Y % LANES
+        value = pltpu.roll(value, shift, 1) if shift else value
+        return jnp.where(in_group(plan, to), value, 0.0)
+
     for a in range(plan.gx):
-        for q in range(plan.own):
-            parts = []
-            label = jnp.zeros((zc, LANES), f32)
+        for q in range(plan.sent):
+            whole, label = [], jnp.zeros((zc, LANES), f32)
             for b in range(plan.gy):
                 start = b * plan.ny
                 values = part(a * plan.gy + b, q)
+                mine = (spot >= start - 1) & (spot <= start + plan.ny)
+                whole.append([jnp.where(mine, v, 0.0) for v in values])
+                if q >= plan.own:
+                    continue
                 second = (values[0] >= 1.5).astype(f32)
                 first = values[0] - 2.0 * second
-                move = start - plan.label_lane(b)
-                first = pltpu.roll(first, move % LANES, 1)
-                second = pltpu.roll(second, (move + 8) % LANES, 1)
+                turn = start - plan.label_lane(b)
+                first = pltpu.roll(first, turn % LANES, 1)
+                second = pltpu.roll(second, (turn + 8) % LANES, 1)
                 label = jnp.where((spot >= start) & (spot < start + 8), first, label)
                 label = jnp.where((spot >= start + 8) & (spot < start + 16), second, label)
-                mine = (spot >= start - 1) & (spot <= start + plan.ny)
-                parts.append([jnp.where(mine, v, 0.0) for v in values])
-                if q == plan.own - 1 and a < plan.gx - 1:
-                    edge = part((a + 1) * plan.gy + b, plan.sent - 1)
-                    parts.append([jnp.where(lane >= LANES - plan.Y, v, 0.0) for v in edge])
-                if q == 0 and a > 0:
-                    edge = part((a - 1) * plan.gy + b, plan.own)
-                    parts.append([jnp.where(lane < plan.Y, v, 0.0) for v in edge])
-            whole, low, high = (functools.reduce(jnp.add, vs) for vs in zip(*parts))
-            tile = a * plan.own + q
-            label_ref[pl.ds(tile, zc, stride=tiles)] = label
-            out_ref[pl.ds(tile, zc, stride=tiles)] = whole
-            out_ref[zc * tiles + tile : zc * tiles + tile + 1] = low
-            out_ref[(zc + 1) * tiles + tile : (zc + 1) * tiles + tile + 1] = high
+            whole = [functools.reduce(jnp.add, vs) for vs in zip(*whole)]
+            ends = jnp.concatenate(whole[1:], axis=0)
+            for n in range(plan.per):
+                if q < plan.own:
+                    x = plan.per * q + n
+                elif plan.shared:
+                    x = {0: plan.nx, plan.per - 1: -1}.get(n)
+                else:
+                    x = plan.nx if q == plan.own else -1
+                if x is None or not 0 <= a * plan.nx + x < plan.X:
+                    continue
+                t, to = place_of(plan, a * plan.nx + x)
+                parts[t].append((move(whole[0], n, to), move(ends, n, to)))
+                if q < plan.own:
+                    labels[t] = labels[t] + move(label, n, to)
+    for t in range(tiles):
+        whole, ends = (functools.reduce(jnp.add, vs) for vs in zip(*parts[t]))
+        label_ref[pl.ds(t, zc, stride=tiles)] = labels[t]
+        out_ref[pl.ds(t, zc, stride=tiles)] = whole
+        out_ref[zc * tiles + t : zc * tiles + t + 1] = ends[0:1]
+        out_ref[(zc + 1) * tiles + t : (zc + 1) * tiles + t + 1] = ends[1:2]
 
     def pack(ref, at, first, count):
         half = -(-count // 2)
@@ -367,36 +396,31 @@
     return s + jnp.log(more) * LOG, small * (1.0 / more)
 
 
-def erode(plan, rank, mask, y_ref, source, result, grown_ref, table_ref, base, first, count):
+def erode(plan, rank, y_ref, source, result, grown_ref, table_ref, base, first, count):
     tiles = slice(8, 8 + plan.tiles)
 
     def body(plane):
         beside = y_neighbours(y_ref, source[pl.ds(plane + base, plan.erode_block), tiles])
         for n in range(plan.erode_block):
             at = plane + n + base
-            cur = source[at, tiles]
-
-            def load(offset, at=at):
-                return source[at, 8 + offset : 8 + offset + plan.tiles]
-
-            total = cur + source[at - 1, tiles] + source[at + 1, tiles]
-            total = total + x_neighbours(plan, mask, load, cur) + beside[n]
+            total = source[at, tiles] + source[at - 1, tiles] + source[at + 1, tiles]
+            total = total + x_neighbours(plan, source, at) + beside[n]
             kind, outside = kind_of(plan, rank, plane + n)
             total = total * table_ref[kind]
-            result[at, tiles] = total
+            wrap(plan, result, at, total)
             grown_ref[at] = 1.0 / (total + outside) - outside
 
     over(first, count, plan.erode_block, body)
 
 
 def spread(plan, y_ref, grown_ref, zy_ref, base, first, count, size):
-    tiles = slice(8, 8 + plan.tiles)
-
     def body(plane):
         at = plane + base
         part = grown_ref[pl.ds(at - 1, size)] + grown_ref[pl.ds(at, size)]
         part = part + grown_ref[pl.ds(at + 1, size)]
-        zy_ref[pl.ds(plane - first, size), tiles] = part + y_neighbours(y_ref, part)
+        part = part + y_neighbours(y_ref, part)
+        for n in range(size):
+            wrap(plan, zy_ref, plane - first + n, part[n])
 
     over(first, count, size, body)
 
@@ -412,13 +436,8 @@
     lax.fori_loop(0, ITERS // 2, pair, 0)
 
 
-def x_box(plan, mask, zy_ref, at):
-    cur = zy_ref[at, 8 : 8 + plan.tiles]
-
-    def load(offset):
-        return zy_ref[at, 8 + offset : 8 + offset + plan.tiles]
-
-    return cur + x_neighbours(plan, mask, load, cur)
+def x_box(plan, zy_ref, at):
+    return zy_ref[at, 8 : 8 + plan.tiles] + x_neighbours(plan, zy_ref, at)
 
 
 def target_kernel(plan, *refs):
@@ -432,7 +451,6 @@
     base = HALO + 1
     tiles = slice(8, 8 + plan.tiles)
     rank = pos_ref[0]
-    mask = masks(plan)
     count_tables(plan, cross_ref, box_ref)
     y_matrix(plan, y_ref)
     e_refs = (e0_ref, e1_ref)
@@ -457,8 +475,9 @@
         for n in range(plan.win_block):
             at = plane + n
             inside = 1.0 - kind_of(plan, rank, at - HALO)[1]
-            out.append((e0_ref, (at + 1, tiles), jnp.exp(-temper * all_ref[at]) * inside))
-        store_all(out)
+            out.append((at + 1, jnp.exp(-temper * all_ref[at]) * inside))
+        for at, value in out:
+            wrap(plan, e0_ref, at, value)
 
     over(0, win, plan.win_block, fill)
 
@@ -467,7 +486,7 @@
         reach = 2 + ITERS - step
         count = zc + 2 * reach
         erode(
-            plan, rank, mask, y_ref, e_ref, e_refs[result], g_ref, cross_ref, base, -reach, count
+            plan, rank, y_ref, e_ref, e_refs[result], g_ref, cross_ref, base, -reach, count
         )
         spread(plan, y_ref, g_ref, zy_ref, base, -1, span, size)
 
@@ -475,7 +494,7 @@
             before = [None if opening else ts_ref[plane + n] for n in range(size)]
             for n in range(size):
                 at = plane + n
-                box = x_box(plan, mask, zy_ref, at)
+                box = x_box(plan, zy_ref, at)
                 kind, outside = kind_of(plan, rank, at - 1)
                 _, _, scaled = thin(e_ref[at - 1 + base, tiles], box, box_ref[kind], outside)
                 ts_ref[at] = scaled * -LOG if opening else lift(scaled, before[n])[0]
@@ -516,7 +535,6 @@
     base, zc, size = plan.base, plan.zc, plan.block
     tiles = slice(8, 8 + plan.tiles)
     rank = pos_ref[0]
-    mask = masks(plan)
 
     for ref in e_refs + g_refs:
         ref[...] = jnp.zeros_like(ref)
@@ -556,9 +574,10 @@
             at = plane + n
             inside = 1.0 - kind_of(plan, rank, at - base)[1]
             predict = sigmoid(e0_ref[at, tiles] + bias_ref[0])
-            out.append((e0_ref, (at, tiles), jnp.exp(-temper * predict) * inside))
-            out.append((g0_ref, at, jnp.exp(temper * predict) * inside))
-        store_all(out)
+            out.append((at, jnp.exp(-temper * predict) * inside))
+            g0_ref[at] = jnp.exp(temper * predict) * inside
+        for at, value in out:
+            wrap(plan, e0_ref, at, value)
 
     over(1, zc + 2 * HALO, plan.erode_block, fill)
 
@@ -571,7 +590,7 @@
         reach = 1 + ITERS - step
         count = zc + 2 * reach
         erode(
-            plan, rank, mask, y_ref, e_ref, e_refs[result], after_ref, cross_ref, base, -reach,
+            plan, rank, y_ref, e_ref, e_refs[result], after_ref, cross_ref, base, -reach,
             count,
         )
         spread(plan, y_ref, after_ref, zy_ref, base, 0, zc, size)
@@ -581,7 +600,7 @@
             before = [None if opening else s_ref[plane + n] for n in range(size)]
             for n in range(size):
                 at = plane + n
-                box = x_box(plan, mask, zy_ref, at)
+                box = x_box(plan, zy_ref, at)
                 kind, outside = kind_of(plan, rank, at)
                 e = e_ref[at + base, tiles]
                 over_box, slope, scaled = thin(e, box, box_ref[kind], outside)
@@ -627,7 +646,6 @@
     rank = pos_ref[0]
     zc, base = plan.zc, plan.pull_base
     tiles = slice(8, 8 + plan.tiles)
-    mask = masks(plan)
 
     def in_copy(left):
         return pltpu.make_async_copy(far_ref.at[left], record_ref.at[left], sem_ref.at[left])
@@ -665,20 +683,23 @@
             size = plan.span_block
             part = push_ref[pl.ds(at, size)] + push_ref[pl.ds(at + 1, size)]
             part = part + push_ref[pl.ds(at + 2, size)]
-            zy_ref[pl.ds(at, size), tiles] = part + y_neighbours(y_ref, part)
+            part = part + y_neighbours(y_ref, part)
+            for n in range(size):
+                wrap(plan, zy_ref, at + n, part[n])
 
         over(0, plan.span, plan.span_block, widen)
 
         def pull(at):
             out = []
             for n in range(plan.span_block):
-                box = x_box(plan, mask, zy_ref, at + n)
+                box = x_box(plan, zy_ref, at + n)
                 inverse = cross_ref[kind_of(plan, rank, at + n - 1)[0]]
                 grown = record_ref[left, at + n + 3 * zc]
                 spot = at + n - 1 + base
                 old = pull_ref[spot, tiles]
-                out.append((pull_ref, (spot, tiles), old - grown * grown * box * inverse))
-            store_all(out)
+                out.append((spot, old - grown * grown * box * inverse))
+            for spot, value in out:
+                wrap(plan, pull_ref, spot, value)
 
         over(0, plan.span, plan.span_block, pull)
         reach = 2 + step
@@ -687,17 +708,11 @@
             beside = y_neighbours(y_ref, pull_ref[pl.ds(plane + base, plan.erode_block), tiles])
             for n in range(plan.erode_block):
                 at = plane + n + base
-                cur = pull_ref[at, tiles]
-
-                def load(offset, at=at):
-                    return pull_ref[at, 8 + offset : 8 + offset + plan.tiles]
-
-                total = cur + pull_ref[at - 1, tiles] + pull_ref[at + 1, tiles]
-                total = total + x_neighbours(plan, mask, load, cur)
-                total = total + beside[n] + wt_ref[at]
+                total = pull_ref[at, tiles] + pull_ref[at - 1, tiles] + pull_ref[at + 1, tiles]
+                total = total + x_neighbours(plan, pull_ref, at) + beside[n] + wt_ref[at]
                 if not ending:
                     total = total * cross_ref[kind_of(plan, rank, plane + n)[0]]
-                next_ref[at, tiles] = total
+                wrap(plan, next_ref, at, total)
 
         over(-reach, zc + 2 * reach, plan.erode_block, join)
 
@@ -764,20 +779,34 @@
             grad_ref[(zc + 1) * plan.tiles + tile : (zc + 1) * plan.tiles + tile + 1],
         ]
 
+    tile_columns = [column(t) for t in range(plan.tiles)]
+
+    def gathered(rows_of):
+        piece = None
+        for n, x in enumerate(rows_of):
+            if x is None or not 0 <= x < plan.X:
+                continue
+            t, group = place_of(plan, x)
+            shift = (n - group) * plan.Y % LANES
+            ends = jnp.concatenate(tile_columns[t][1:], axis=0)
+            values = [tile_columns[t][0], ends]
+            if shift:
+                values = [pltpu.roll(v, shift, 1) for v in values]
+            values = [jnp.where(in_group(plan, n), v, 0.0) for v in values]
+            piece = values if piece is None else [x + y for x, y in zip(piece, values)]
+        if piece is None:
+            piece = [jnp.zeros((zc, LANES), f32), jnp.zeros((2, LANES), f32)]
+        return [piece[0], piece[1][0:1], piece[1][1:2]]
+
     for a in range(plan.gx):
-        pieces = [column(a * plan.own + q) for q in range(plan.own)]
-        zero = [jnp.zeros((zc, LANES), f32)] + [jnp.zeros((1, LANES), f32)] * 2
-        after = column((a + 1) * plan.own) if a < plan.gx - 1 else zero
-        before = column(a * plan.own - 1) if a > 0 else zero
+        first, per = a * plan.nx, plan.per
+        pieces = [
+            gathered([first + per * q + n for n in range(per)]) for q in range(plan.own)
+        ]
         if plan.shared:
-            pieces.append(
-                [
-                    jnp.where(lane < plan.Y, x, 0.0) + jnp.where(lane >= LANES - plan.Y, y, 0.0)
-                    for x, y in zip(after, before)
-                ]
-            )
+            pieces.append(gathered([first + plan.nx] + [None] * (per - 2) + [first - 1]))
         else:
-            pieces += [after, before]
+            pieces += [gathered([first + plan.nx]), gathered([first - 1])]
         edges = [edge for piece in pieces for edge in piece[1:]]
         rows = plan.R16
         edges += [jnp.zeros((1, LANES), f32)] * (plan.extra16 * rows - len(edges))

time: 110 us -> 120 us (1.091)
  Pallas kernels: 50.3 us -> 59.6 us
    pallas_call x10, Pallas kernels: 50.3 us -> 59.6 us  [call(): pl.pallas_call(functools.partial(kernel, plan), out_shape=out_shape, in_s...]
  transfers between devices with their start and end apart: 7 -> 7, of which waited for: 3 -> 3; matrix products, arithmetic and copies ran while one was open for 1% -> 1% of each run, Pallas kernels for 25% -> 28%
where the time goes in v1:
time: 120 us; the launch traced here: 119 us
  Pallas kernels  59.6 us (50%)
  starting transfers between devices  25.2 us (21%)
  blocking collectives  24.4 us (20%)
  waiting for transfers between devices  7.71 us (6%)
  between operations  1.45 us (1%)
    pallas_call x10, Pallas kernels, call(): pl.pallas_call(functools.partial(kernel, plan), out_shape=out_shape, in_s...  59.6 us
    all_to_all x2, blocking collectives, exchange(): return lax.all_to_all(array, GROUP, 0, 0, tiled=True)  24.4 us
    all_to_all x3, starting transfers between devices, everywhere(): return lax.all_to_all(array, ALL_AXES, 0, 0, tiled=True)  18.3 us
    ppermute x4, starting transfers between devices, hop(): return lax.ppermute(array, ALL_AXES, pairs)  6.84 us
    ppermute x4, waiting for transfers between devices, hop(): return lax.ppermute(array, ALL_AXES, pairs)  4.55 us
    all_to_all x3, waiting for transfers between devices, everywhere(): return lax.all_to_all(array, ALL_AXES, 0, 0, tiled=True)  3.17 us
  transfers between devices with their start and end apart: 7, of which 3 were waited for; matrix products, arithmetic and copies ran while one was open for 1% of the time, Pallas kernels for 28%

profile of v1, /device:TPU:0, one launch (start us, length us, event | category | flops | bytes accessed | tf_op | source)
XLA Modules:
  0.0 119.0 jit_solution(766561815096076631)
XLA Ops:
  0.7 0.1 pad_add_fusion.pos_ref.refs_0_
  0.7 3.6 %shard_map.75 = f32[8,6,16,128]{3,2,1,0:T(8,128)S(1)} custom-call(s32[2]{0:T(128)S(1)} %pad_add_fusion.pos_ref.refs_0_, bf16[27,32]{1,0:T(8,128)(2,1)} %w_ref.1, bf16[32,16,16,128]{3,2,1,0:T(8,128)(2,1)} %far_ref.3, s32[16,16,128]{2,1,0:T(8,128)} %label_ref.1), custom_call_target="tpu_custom_call" | custom-call | bytes 175000 | tf_op jit(solution)/shard_map/pallas_call | solution.py:986
  4.3 12.8 %all_to_all.25.got_ref = f32[8,6,16,128]{3,2,1,0:T(8,128)S(1)} all-to-all(f32[8,6,16,128]{3,2,1,0:T(8,128)S(1)} %shard_map.75), channel_id=1, replica_groups=mesh['gx'=4,'gy'=2,'gz'=4] {'gx','gy'}, dimensions={0} | all-to-all | bytes 786432 | tf_op jit(solution)/shard_map/all_to_all | solution.py:996
  17.1 1.2 shard_map.76
  18.3 2.1 %collective-permute-start = (f32[21,16,128]{2,1,0:T(8,128)S(1)}, f32[21,16,128]{2,1,0:T(8,128)S(1)}, u32[]{:S(2)}, u32[]{:S(2)}) collective-permute-start(f32[21,16,128]{2,1,0:T(8,128)S(1)} %bitcast.15), channel_id=1, source_target_pairs={{0,8},{8,16},{16,24},{24,28},{28,20},{20,12},{12,4},{4,5},{5,13},{... | collective-permute-start | bytes 516104 | tf_op jit(solution)/shard_map/ppermute | solution.py:1011
  20.4 1.3 %collective-permute-start.1 = (f32[21,16,128]{2,1,0:T(8,128)S(1)}, f32[21,16,128]{2,1,0:T(8,128)S(1)}, u32[]{:S(2)}, u32[]{:S(2)}) collective-permute-start(f32[21,16,128]{2,1,0:T(8,128)S(1)} %bitcast.14), channel_id=1, source_target_pairs={{8,0},{16,8},{24,16},{28,24},{20,28},{12,20},{4,12},{5,4},{13,5},{... | collective-permute-start | bytes 516104 | tf_op jit(solution)/shard_map/ppermute | solution.py:1011
  22.3 0.0 collective-permute-done.refs_4_.refs_3_
  22.3 1.5 %collective-permute-done.1.refs_5_.refs_4_ = f32[21,16,128]{2,1,0:T(8,128)S(1)} collective-permute-done((f32[21,16,128]{2,1,0:T(8,128)S(1)}, f32[21,16,128]{2,1,0:T(8,128)S(1)}, u32[]{:S(2)}, u32[]{:S(2)}) %collective-permute-start.1) | collective-permute-done | bytes 172064 | tf_op jit(solution)/shard_map/ppermute | solution.py:1011
  23.9 15.8 %shard_map.77 = (f32[11,66,16,128]{3,2,1,0:T(8,128)}, f32[18,16,128]{2,1,0:T(8,128)S(1)}, f32[32,8,128]{2,1,0:T(8,128)}) custom-call(s32[2]{0:T(128)S(1)} %pad_add_fusion.pos_ref.refs_0_, f32[1]{0:T(128)S(6)} %copy.9.refs_1_, f32[16,16,128]{2,1,0:T(8,128)S(1)} %bitcast.9, f32[26,16,128]{2,1,0:T(8,128)S(1)} %bitcast.12, ...), custom_call_target="tpu_custom_call" | custom-call | bytes 275000 | tf_op jit(solution)/shard_map/pallas_call | solution.py:986
  39.7 8.7 %all-to-all-start.1 = ((f32[32,8,128]{2,1,0:T(8,128)}), f32[32,8,128]{2,1,0:T(8,128)S(1)}, u32[]{:S(2)}, u32[]{:S(2)}) async-start(f32[32,8,128]{2,1,0:T(8,128)} %get-tuple-element.28), calls=%async_computation.1 | async-start | bytes 262144 | tf_op jit(solution)/shard_map/all_to_all | solution.py:999
  48.4 14.8 %shard_map.78 = (f32[18,16,128]{2,1,0:T(8,128)S(1)}, f32[18,16,128]{2,1,0:T(8,128)S(1)}, f32[32,8,128]{2,1,0:T(8,128)}) custom-call(s32[2]{0:T(128)S(1)} %pad_add_fusion.pos_ref.refs_0_, f32[18,16,128]{2,1,0:T(8,128)S(1)} %get-tuple-element.29.refs_1_.refs_3_, f32[16,16,128]{2,1,0:T(8,128)S(1)} %bitcast.10, ...), custom_call_target="tpu_custom_call" | custom-call | bytes 325000 | tf_op jit(solution)/shard_map/pallas_call | solution.py:986
  63.2 0.0 all-to-all-done.1.refs_1_
  63.2 5.8 %all-to-all-start.2 = ((f32[32,8,128]{2,1,0:T(8,128)}), f32[32,8,128]{2,1,0:T(8,128)S(1)}, u32[]{:S(2)}, u32[]{:S(2)}) async-start(f32[32,8,128]{2,1,0:T(8,128)} %get-tuple-element.30), calls=%async_computation.2 | async-start | bytes 262144 | tf_op jit(solution)/shard_map/all_to_all | solution.py:999
  69.1 14.5 %shard_map.79 = (f32[18,16,128]{2,1,0:T(8,128)S(1)}, f32[13,16,128]{2,1,0:T(8,128)S(1)}, f32[13,16,128]{2,1,0:T(8,128)S(1)}) custom-call(s32[2]{0:T(128)S(1)} %pad_add_fusion.pos_ref.refs_0_, f32[32,8,128]{2,1,0:T(8,128)S(1)} %all-to-all-done.1.refs_1_, f32[16,16,128]{2,1,0:T(8,128)S(1)} %bitcast.11, f32[11,66,16,128]{3,2,1,0:T(8,128)} %get-tuple-element.33.refs_3_), custom_call_target="tpu_custom_call" | custom-call | bytes 275000 | tf_op jit(solution)/shard_map/pallas_call | solution.py:986
  83.6 0.0 copy-start
  83.7 2.2 %collective-permute-start.2 = (f32[13,16,128]{2,1,0:T(8,128)S(1)}, f32[13,16,128]{2,1,0:T(8,128)S(1)}, u32[]{:S(2)}, u32[]{:S(2)}) collective-permute-start(f32[13,16,128]{2,1,0:T(8,128)S(1)} %get-tuple-element.35), channel_id=1, source_target_pairs={{0,8},{8,16},{16,24},{24,28},{28,20},{20,12},{12,4},{4,5},{5,13},{... | collective-permute-start | bytes 319496 | tf_op jit(solution)/shard_map/ppermute | solution.py:1011
  85.8 1.3 %collective-permute-start.3 = (f32[13,16,128]{2,1,0:T(8,128)S(1)}, f32[13,16,128]{2,1,0:T(8,128)S(1)}, u32[]{:S(2)}, u32[]{:S(2)}) collective-permute-start(f32[13,16,128]{2,1,0:T(8,128)S(1)} %get-tuple-element.36), channel_id=1, source_target_pairs={{8,0},{16,8},{24,16},{28,24},{20,28},{12,20},{4,12},{5,4},{13,5},{... | collective-permute-start | bytes 319496 | tf_op jit(solution)/shard_map/ppermute | solution.py:1011
  87.1 0.0 all-to-all-done.2.refs_2_
  87.1 0.0 collective-permute-done.2.refs_7_
  87.1 3.0 %collective-permute-done.3.refs_8_ = f32[13,16,128]{2,1,0:T(8,128)S(1)} collective-permute-done((f32[13,16,128]{2,1,0:T(8,128)S(1)}, f32[13,16,128]{2,1,0:T(8,128)S(1)}, u32[]{:S(2)}, u32[]{:S(2)}) %collective-permute-start.3) | collective-permute-done | bytes 106528 | tf_op jit(solution)/shard_map/ppermute | solution.py:1011
  90.2 1.0 shard_map.80
  91.1 11.6 %all_to_all.26.got_ref = bf16[8,6,16,128]{3,2,1,0:T(8,128)(2,1)S(1)} all-to-all(bf16[8,6,16,128]{3,2,1,0:T(8,128)(2,1)S(1)} %get-tuple-element.39), channel_id=1, replica_groups=mesh['gx'=4,'gy'=2,'gz'=4] {'gx','gy'}, dimensions={0} | all-to-all | bytes 393216 | tf_op jit(solution)/shard_map/all_to_all | solution.py:996
  102.7 4.0 %shard_map.82 = (f32[32,8,128]{2,1,0:T(8,128)}, bf16[18,96,128]{2,1,0:T(8,128)(2,1)S(1)}) custom-call(s32[2]{0:T(128)S(1)} %pad_add_fusion.pos_ref.refs_0_, bf16[32,16,16,128]{3,2,1,0:T(8,128)(2,1)} %far_ref.3, f32[8,128]{1,0:T(8,128)S(1)} %get-tuple-element.38.bias_ref, bf16[8,6,16,128]{3,2,1,0:T(8,128)(2,1)S(1)} %all_to_all.26.got_ref), custom_call_target="tpu_custom_call" | custom-call | bytes 125000 | tf_op jit(solution)/shard_map/pallas_call | solution.py:986
  106.7 3.8 %all-to-all-start.4 = ((f32[32,8,128]{2,1,0:T(8,128)}), f32[32,8,128]{2,1,0:T(8,128)S(1)}, u32[]{:S(2)}, u32[]{:S(2)}) async-start(f32[32,8,128]{2,1,0:T(8,128)} %get-tuple-element.41.after_ref), calls=%async_computation.4 | async-start | bytes 262144 | tf_op jit(solution)/shard_map/all_to_all | solution.py:999
  110.5 0.0 copy-done
  110.5 0.1 copy.8
  110.6 1.4 %shard_map.81.wide_ref = bf16[512,288]{1,0:T(8,128)(2,1)S(1)} custom-call(s32[2]{0:T(128)S(1)} %pad_add_fusion.pos_ref.refs_0_, bf16[32,27]{1,0:T(8,128)(2,1)S(1)} %bitcast.13, f32[18,16,128]{2,1,0:T(8,128)S(1)} %get-tuple-element.34.refs_6_.after_ref), custom_call_target="tpu_custom_call" | custom-call | bytes 50000 | tf_op jit(solution)/shard_map/pallas_call | solution.py:986
  112.1 0.5 slice.3
  112.6 2.6 %shard_map.83 = bf16[32,16,16,128]{3,2,1,0:T(8,128)(2,1)} custom-call(bf16[512,288]{1,0:T(8,128)(2,1)S(1)} %shard_map.81.wide_ref, bf16[18,96,128]{2,1,0:T(8,128)(2,1)S(1)} %get-tuple-element.40.g_ref, f32[32,8,128]{2,1,0:T(8,128)} %get-tuple-element.41.after_ref), custom_call_target="tpu_custom_call" | custom-call | bytes 125000 | tf_op jit(solution)/shard_map/pallas_call | solution.py:986
  115.2 3.2 %all-to-all-done.4.got_ref = f32[32,8,128]{2,1,0:T(8,128)S(1)} async-done(((f32[32,8,128]{2,1,0:T(8,128)}), f32[32,8,128]{2,1,0:T(8,128)S(1)}, u32[]{:S(2)}, u32[]{:S(2)}) %all-to-all-start.4) | async-done | bytes 131104 | tf_op jit(solution)/shard_map/all_to_all | solution.py:999
  118.3 0.7 shard_map.84
Async XLA Ops:
  18.3 4.0 %collective-permute-start = (f32[21,16,128]{2,1,0:T(8,128)S(1)}, f32[21,16,128]{2,1,0:T(8,128)S(1)}, u32[]{:S(2)}, u32[]{:S(2)}) collective-permute-start(f32[21,16,128]{2,1,0:T(8,128)S(1)} %bitcast.15), channel_id=1, source_target_pairs={{0,8},{8,16},{16,24},{24,28},{28,20},{20,12},{12,4},{4,5},{5,13},{... | collective-permute-start | bytes 516104 | tf_op jit(solution)/shard_map/ppermute | solution.py:1011
  20.4 3.5 %collective-permute-start.1 = (f32[21,16,128]{2,1,0:T(8,128)S(1)}, f32[21,16,128]{2,1,0:T(8,128)S(1)}, u32[]{:S(2)}, u32[]{:S(2)}) collective-permute-start(f32[21,16,128]{2,1,0:T(8,128)S(1)} %bitcast.14), channel_id=1, source_target_pairs={{8,0},{16,8},{24,16},{28,24},{20,28},{12,20},{4,12},{5,4},{13,5},{... | collective-permute-start | bytes 516104 | tf_op jit(solution)/shard_map/ppermute | solution.py:1011
  39.7 23.5 %all-to-all-start.1 = ((f32[32,8,128]{2,1,0:T(8,128)}), f32[32,8,128]{2,1,0:T(8,128)S(1)}, u32[]{:S(2)}, u32[]{:S(2)}) async-start(f32[32,8,128]{2,1,0:T(8,128)} %get-tuple-element.28), calls=%async_computation.1 | async-start | bytes 262144 | tf_op jit(solution)/shard_map/all_to_all | solution.py:999
  63.2 23.9 %all-to-all-start.2 = ((f32[32,8,128]{2,1,0:T(8,128)}), f32[32,8,128]{2,1,0:T(8,128)S(1)}, u32[]{:S(2)}, u32[]{:S(2)}) async-start(f32[32,8,128]{2,1,0:T(8,128)} %get-tuple-element.30), calls=%async_computation.2 | async-start | bytes 262144 | tf_op jit(solution)/shard_map/all_to_all | solution.py:999
  83.6 26.9 %copy-start = (bf16[27,32]{1,0:T(8,128)(2,1)S(1)}, bf16[27,32]{1,0:T(8,128)(2,1)}, u32[]{:S(2)}) copy-start(bf16[27,32]{1,0:T(8,128)(2,1)} %w_ref.1) | copy-start | bytes 5188
  83.7 3.5 %collective-permute-start.2 = (f32[13,16,128]{2,1,0:T(8,128)S(1)}, f32[13,16,128]{2,1,0:T(8,128)S(1)}, u32[]{:S(2)}, u32[]{:S(2)}) collective-permute-start(f32[13,16,128]{2,1,0:T(8,128)S(1)} %get-tuple-element.35), channel_id=1, source_target_pairs={{0,8},{8,16},{16,24},{24,28},{28,20},{20,12},{12,4},{4,5},{5,13},{... | collective-permute-start | bytes 319496 | tf_op jit(solution)/shard_map/ppermute | solution.py:1011
  85.8 4.3 %collective-permute-start.3 = (f32[13,16,128]{2,1,0:T(8,128)S(1)}, f32[13,16,128]{2,1,0:T(8,128)S(1)}, u32[]{:S(2)}, u32[]{:S(2)}) collective-permute-start(f32[13,16,128]{2,1,0:T(8,128)S(1)} %get-tuple-element.36), channel_id=1, source_target_pairs={{8,0},{16,8},{24,16},{28,24},{20,28},{12,20},{4,12},{5,4},{13,5},{... | collective-permute-start | bytes 319496 | tf_op jit(solution)/shard_map/ppermute | solution.py:1011
  106.7 11.6 %all-to-all-start.4 = ((f32[32,8,128]{2,1,0:T(8,128)}), f32[32,8,128]{2,1,0:T(8,128)S(1)}, u32[]{:S(2)}, u32[]{:S(2)}) async-start(f32[32,8,128]{2,1,0:T(8,128)} %get-tuple-element.41.after_ref), calls=%async_computation.4 | async-start | bytes 262144 | tf_op jit(solution)/shard_map/all_to_all | solution.py:999

commit v2 on v0

--- a/solution.py
+++ b/solution.py
@@ -518,7 +518,7 @@
     rank = pos_ref[0]
     mask = masks(plan)
 
-    for ref in e_refs + g_refs:
+    for ref in e_refs:
         ref[...] = jnp.zeros_like(ref)
     zy_ref[...] = jnp.zeros_like(zy_ref)
     count_tables(plan, cross_ref, box_ref)
@@ -795,9 +795,8 @@
 
 
 def weight_kernel(
-    plan, pos_ref, far_ref, bias_ref, got_ref, gw_ref, g_ref, dw_ref, f_ref, sem_ref
+    plan, pos_ref, f_ref, bias_ref, got_ref, gw_ref, g_ref, dw_ref
 ):
-    copies = stream(plan, far_ref, f_ref, sem_ref)
     rows, inner = plan.Y, plan.ch * plan.ny
     zc, nz = plan.zc, plan.nz
     lane = lane_iota((rows, nz))
@@ -826,7 +825,6 @@
 
     width = plan.nx // PARTS
     for n in range(PARTS):
-        copies[n].wait()
         dw_ref[...] += lax.dot_general(
             moved_columns(g_ref, n * width, width),
             columns(plan, f_ref, n * width, width),
@@ -947,7 +945,7 @@
     x, y, z = (lax.axis_index(axis).astype(jnp.int32) for axis in ALL_AXES)
     mine = y * plan.gx + jnp.where(y % 2 == 0, x, plan.gx - 1 - x)
     place = z * members + jnp.where(z % 2 == 0, mine, members - 1 - mine)
-    pos = jnp.stack([place, y])
+    pos = pltpu.with_memory_space_constraint(jnp.stack([place, y]), pltpu.HBM)
 
     def call(
         kernel, out_shape, in_specs, operands, micros, scratch=(), out_specs=None
@@ -981,7 +979,8 @@
         ]
         return lax.ppermute(array, ALL_AXES, pairs)
 
-    turned = weight.T
+    turned = pltpu.with_memory_space_constraint(weight.T, pltpu.HBM)
+    features_ahead = features
     features, weight, label = (
         pltpu.with_memory_space_constraint(a, pltpu.HBM) for a in (features, weight, label)
     )
@@ -1119,10 +1118,10 @@
     partial, g = call(
         weight_kernel,
         [shape((plan.ranks, 8, LANES)), moved],
-        [SMEM, FAR, VMEM, VMEM],
-        (pos, features, bias_part, exchange(grad_sent)),
+        [SMEM, VMEM, VMEM, VMEM],
+        (pos, features_ahead, bias_part, exchange(grad_sent)),
         5,
-        [pltpu.VMEM((bands, inner), f32)] + features_near,
+        [pltpu.VMEM((bands, inner), f32)],
     )
     grad_features = call(
         feature_kernel,

time: 110 us -> 110 us (level)
  transfers between devices with their start and end apart: 7 -> 7, of which waited for: 3 -> 3; matrix products, arithmetic and copies ran while one was open for 1% -> 1% of each run, Pallas kernels for 25% -> 26%
where the time goes in v2:
time: 110 us
  Pallas kernels  49.8 us (45%)
  starting transfers between devices  25.2 us (23%)
  blocking collectives  24.4 us (22%)
  waiting for transfers between devices  6.96 us (6%)
  between operations  1.45 us (1%)
  local copies, waits for them, and re-layouts  1.21 us (1%)
    pallas_call x10, Pallas kernels, call(): pl.pallas_call(functools.partial(kernel, plan), out_shape=out_shape, in_s...  49.8 us
    all_to_all x2, blocking collectives, exchange(): return lax.all_to_all(array, GROUP, 0, 0, tiled=True)  24.4 us
    all_to_all x3, starting transfers between devices, everywhere(): return lax.all_to_all(array, ALL_AXES, 0, 0, tiled=True)  18.3 us
    ppermute x4, starting transfers between devices, hop(): return lax.ppermute(array, ALL_AXES, pairs)  6.83 us
    ppermute x4, waiting for transfers between devices, hop(): return lax.ppermute(array, ALL_AXES, pairs)  4.55 us
    all_to_all x3, waiting for transfers between devices, everywhere(): return lax.all_to_all(array, ALL_AXES, 0, 0, tiled=True)  2.42 us
  transfers between devices with their start and end apart: 7, of which 3 were waited for; matrix products, arithmetic and copies ran while one was open for 1% of the time, Pallas kernels for 26%

profile of v2, /device:TPU:0, one launch (start us, length us, event | category | flops | bytes accessed | tf_op | source)
XLA Modules:
  0.0 109.6 jit_solution(9084287391490388514)
XLA Ops:
  0.7 0.6 pad_add_fusion.pos_ref.refs_0_
  1.3 3.6 %shard_map.75 = f32[8,6,16,128]{3,2,1,0:T(8,128)S(1)} custom-call(s32[2]{0:T(128)} %pad_add_fusion.pos_ref.refs_0_, bf16[27,32]{1,0:T(8,128)(2,1)} %w_ref.1, bf16[32,16,16,128]{3,2,1,0:T(8,128)(2,1)} %f_ref.1, s32[16,16,128]{2,1,0:T(8,128)} %label_ref.1), custom_call_target="tpu_custom_call" | custom-call | bytes 175000 | tf_op jit(solution)/shard_map/pallas_call | solution.py:955
  4.9 12.8 %all_to_all.25.got_ref = f32[8,6,16,128]{3,2,1,0:T(8,128)S(1)} all-to-all(f32[8,6,16,128]{3,2,1,0:T(8,128)S(1)} %shard_map.75), channel_id=1, replica_groups=mesh['gx'=4,'gy'=2,'gz'=4] {'gx','gy'}, dimensions={0} | all-to-all | bytes 786432 | tf_op jit(solution)/shard_map/all_to_all | solution.py:965
  17.7 0.2 shard_map.76
  17.9 2.1 %collective-permute-start = (f32[21,16,128]{2,1,0:T(8,128)S(1)}, f32[21,16,128]{2,1,0:T(8,128)S(1)}, u32[]{:S(2)}, u32[]{:S(2)}) collective-permute-start(f32[21,16,128]{2,1,0:T(8,128)S(1)} %bitcast.14), channel_id=1, source_target_pairs={{0,8},{8,16},{16,24},{24,28},{28,20},{20,12},{12,4},{4,5},{5,13},{... | collective-permute-start | bytes 516104 | tf_op jit(solution)/shard_map/ppermute | solution.py:980
  20.0 1.3 %collective-permute-start.1 = (f32[21,16,128]{2,1,0:T(8,128)S(1)}, f32[21,16,128]{2,1,0:T(8,128)S(1)}, u32[]{:S(2)}, u32[]{:S(2)}) collective-permute-start(f32[21,16,128]{2,1,0:T(8,128)S(1)} %bitcast.13), channel_id=1, source_target_pairs={{8,0},{16,8},{24,16},{28,24},{20,28},{12,20},{4,12},{5,4},{13,5},{... | collective-permute-start | bytes 516104 | tf_op jit(solution)/shard_map/ppermute | solution.py:980
  22.0 0.0 collective-permute-done.refs_4_.refs_3_
  22.0 1.5 %collective-permute-done.1.refs_5_.refs_4_ = f32[21,16,128]{2,1,0:T(8,128)S(1)} collective-permute-done((f32[21,16,128]{2,1,0:T(8,128)S(1)}, f32[21,16,128]{2,1,0:T(8,128)S(1)}, u32[]{:S(2)}, u32[]{:S(2)}) %collective-permute-start.1) | collective-permute-done | bytes 172064 | tf_op jit(solution)/shard_map/ppermute | solution.py:980
  23.5 13.3 %shard_map.77 = (f32[11,66,16,128]{3,2,1,0:T(8,128)}, f32[18,16,128]{2,1,0:T(8,128)S(1)}, f32[32,8,128]{2,1,0:T(8,128)}) custom-call(s32[2]{0:T(128)} %pad_add_fusion.pos_ref.refs_0_, f32[1]{0:T(128)S(6)} %copy.9.refs_1_, f32[16,16,128]{2,1,0:T(8,128)S(1)} %bitcast.9, f32[26,16,128]{2,1,0:T(8,128)S(1)} %bitcast.12, ...), custom_call_target="tpu_custom_call" | custom-call | bytes 275000 | tf_op jit(solution)/shard_map/pallas_call | solution.py:955
  36.8 8.7 %all-to-all-start.1 = ((f32[32,8,128]{2,1,0:T(8,128)}), f32[32,8,128]{2,1,0:T(8,128)S(1)}, u32[]{:S(2)}, u32[]{:S(2)}) async-start(f32[32,8,128]{2,1,0:T(8,128)} %get-tuple-element.28), calls=%async_computation.1 | async-start | bytes 262144 | tf_op jit(solution)/shard_map/all_to_all | solution.py:968
  45.5 12.4 %shard_map.78 = (f32[18,16,128]{2,1,0:T(8,128)S(1)}, f32[18,16,128]{2,1,0:T(8,128)S(1)}, f32[32,8,128]{2,1,0:T(8,128)}) custom-call(s32[2]{0:T(128)} %pad_add_fusion.pos_ref.refs_0_, f32[18,16,128]{2,1,0:T(8,128)S(1)} %get-tuple-element.29.refs_1_.refs_3_, f32[16,16,128]{2,1,0:T(8,128)S(1)} %bitcast.10, ...), custom_call_target="tpu_custom_call" | custom-call | bytes 325000 | tf_op jit(solution)/shard_map/pallas_call | solution.py:955
  57.9 0.0 all-to-all-done.1.refs_1_
  57.9 5.8 %all-to-all-start.2 = ((f32[32,8,128]{2,1,0:T(8,128)}), f32[32,8,128]{2,1,0:T(8,128)S(1)}, u32[]{:S(2)}, u32[]{:S(2)}) async-start(f32[32,8,128]{2,1,0:T(8,128)} %get-tuple-element.30), calls=%async_computation.2 | async-start | bytes 262144 | tf_op jit(solution)/shard_map/all_to_all | solution.py:968
  63.8 0.0 copy-start
  63.8 11.7 %shard_map.79 = (f32[18,16,128]{2,1,0:T(8,128)S(1)}, f32[13,16,128]{2,1,0:T(8,128)S(1)}, f32[13,16,128]{2,1,0:T(8,128)S(1)}) custom-call(s32[2]{0:T(128)} %pad_add_fusion.pos_ref.refs_0_, f32[32,8,128]{2,1,0:T(8,128)S(1)} %all-to-all-done.1.refs_1_, f32[16,16,128]{2,1,0:T(8,128)S(1)} %bitcast.11, f32[11,66,16,128]{3,2,1,0:T(8,128)} %get-tuple-element.33.refs_3_), custom_call_target="tpu_custom_call" | custom-call | bytes 275000 | tf_op jit(solution)/shard_map/pallas_call | solution.py:955
  75.5 0.0 copy-start.1
  75.5 2.2 %collective-permute-start.2 = (f32[13,16,128]{2,1,0:T(8,128)S(1)}, f32[13,16,128]{2,1,0:T(8,128)S(1)}, u32[]{:S(2)}, u32[]{:S(2)}) collective-permute-start(f32[13,16,128]{2,1,0:T(8,128)S(1)} %get-tuple-element.35), channel_id=1, source_target_pairs={{0,8},{8,16},{16,24},{24,28},{28,20},{20,12},{12,4},{4,5},{5,13},{... | collective-permute-start | bytes 319496 | tf_op jit(solution)/shard_map/ppermute | solution.py:980
  77.7 1.3 %collective-permute-start.3 = (f32[13,16,128]{2,1,0:T(8,128)S(1)}, f32[13,16,128]{2,1,0:T(8,128)S(1)}, u32[]{:S(2)}, u32[]{:S(2)}) collective-permute-start(f32[13,16,128]{2,1,0:T(8,128)S(1)} %get-tuple-element.36), channel_id=1, source_target_pairs={{8,0},{16,8},{24,16},{28,24},{20,28},{12,20},{4,12},{5,4},{13,5},{... | collective-permute-start | bytes 319496 | tf_op jit(solution)/shard_map/ppermute | solution.py:980
  79.0 0.0 all-to-all-done.2.refs_2_
  79.0 0.0 collective-permute-done.2.refs_7_
  79.0 3.0 %collective-permute-done.3.refs_8_ = f32[13,16,128]{2,1,0:T(8,128)S(1)} collective-permute-done((f32[13,16,128]{2,1,0:T(8,128)S(1)}, f32[13,16,128]{2,1,0:T(8,128)S(1)}, u32[]{:S(2)}, u32[]{:S(2)}) %collective-permute-start.3) | collective-permute-done | bytes 106528 | tf_op jit(solution)/shard_map/ppermute | solution.py:980
  82.0 0.9 shard_map.80
  83.0 11.6 %all_to_all.26.got_ref = bf16[8,6,16,128]{3,2,1,0:T(8,128)(2,1)S(1)} all-to-all(bf16[8,6,16,128]{3,2,1,0:T(8,128)(2,1)S(1)} %get-tuple-element.39), channel_id=1, replica_groups=mesh['gx'=4,'gy'=2,'gz'=4] {'gx','gy'}, dimensions={0} | all-to-all | bytes 393216 | tf_op jit(solution)/shard_map/all_to_all | solution.py:965
  94.6 0.0 copy-done
  94.6 2.8 %shard_map.82 = (f32[32,8,128]{2,1,0:T(8,128)}, bf16[18,96,128]{2,1,0:T(8,128)(2,1)S(1)}) custom-call(s32[2]{0:T(128)} %pad_add_fusion.pos_ref.refs_0_, bf16[32,16,16,128]{3,2,1,0:T(8,128)(2,1)S(1)} %copy-done, f32[8,128]{1,0:T(8,128)S(1)} %get-tuple-element.38.bias_ref, bf16[8,6,16,128]{3,2,1,0:T(8,128)(2,1)S(1)} %all_to_all.26.got_ref), custom_call_target="tpu_custom_call" | custom-call | bytes 125000 | tf_op jit(solution)/shard_map/pallas_call | solution.py:955
  97.3 3.8 %all-to-all-start.4 = ((f32[32,8,128]{2,1,0:T(8,128)}), f32[32,8,128]{2,1,0:T(8,128)S(1)}, u32[]{:S(2)}, u32[]{:S(2)}) async-start(f32[32,8,128]{2,1,0:T(8,128)} %get-tuple-element.41.after_ref), calls=%async_computation.4 | async-start | bytes 262144 | tf_op jit(solution)/shard_map/all_to_all | solution.py:968
  101.1 0.0 copy-done.1
  101.1 0.7 copy.8
  101.8 1.6 %shard_map.81.wide_ref = bf16[512,288]{1,0:T(8,128)(2,1)S(1)} custom-call(s32[2]{0:T(128)} %pad_add_fusion.pos_ref.refs_0_, bf16[32,27]{1,0:T(8,128)(2,1)} %bitcast.15, f32[18,16,128]{2,1,0:T(8,128)S(1)} %get-tuple-element.34.refs_6_.after_ref), custom_call_target="tpu_custom_call" | custom-call | bytes 50000 | tf_op jit(solution)/shard_map/pallas_call | solution.py:955
  103.4 0.5 slice.3
  103.9 2.6 %shard_map.83 = bf16[32,16,16,128]{3,2,1,0:T(8,128)(2,1)} custom-call(bf16[512,288]{1,0:T(8,128)(2,1)S(1)} %shard_map.81.wide_ref, bf16[18,96,128]{2,1,0:T(8,128)(2,1)S(1)} %get-tuple-element.40.g_ref, f32[32,8,128]{2,1,0:T(8,128)} %get-tuple-element.41.after_ref), custom_call_target="tpu_custom_call" | custom-call | bytes 125000 | tf_op jit(solution)/shard_map/pallas_call | solution.py:955
  106.5 2.4 %all-to-all-done.4.got_ref = f32[32,8,128]{2,1,0:T(8,128)S(1)} async-done(((f32[32,8,128]{2,1,0:T(8,128)}), f32[32,8,128]{2,1,0:T(8,128)S(1)}, u32[]{:S(2)}, u32[]{:S(2)}) %all-to-all-start.4) | async-done | bytes 131104 | tf_op jit(solution)/shard_map/all_to_all | solution.py:968
  108.9 0.7 shard_map.84
Async XLA Ops:
  17.9 4.0 %collective-permute-start = (f32[21,16,128]{2,1,0:T(8,128)S(1)}, f32[21,16,128]{2,1,0:T(8,128)S(1)}, u32[]{:S(2)}, u32[]{:S(2)}) collective-permute-start(f32[21,16,128]{2,1,0:T(8,128)S(1)} %bitcast.14), channel_id=1, source_target_pairs={{0,8},{8,16},{16,24},{24,28},{28,20},{20,12},{12,4},{4,5},{5,13},{... | collective-permute-start | bytes 516104 | tf_op jit(solution)/shard_map/ppermute | solution.py:980
  20.0 3.5 %collective-permute-start.1 = (f32[21,16,128]{2,1,0:T(8,128)S(1)}, f32[21,16,128]{2,1,0:T(8,128)S(1)}, u32[]{:S(2)}, u32[]{:S(2)}) collective-permute-start(f32[21,16,128]{2,1,0:T(8,128)S(1)} %bitcast.13), channel_id=1, source_target_pairs={{8,0},{16,8},{24,16},{28,24},{20,28},{12,20},{4,12},{5,4},{13,5},{... | collective-permute-start | bytes 516104 | tf_op jit(solution)/shard_map/ppermute | solution.py:980
  36.8 21.1 %all-to-all-start.1 = ((f32[32,8,128]{2,1,0:T(8,128)}), f32[32,8,128]{2,1,0:T(8,128)S(1)}, u32[]{:S(2)}, u32[]{:S(2)}) async-start(f32[32,8,128]{2,1,0:T(8,128)} %get-tuple-element.28), calls=%async_computation.1 | async-start | bytes 262144 | tf_op jit(solution)/shard_map/all_to_all | solution.py:968
  57.9 21.0 %all-to-all-start.2 = ((f32[32,8,128]{2,1,0:T(8,128)}), f32[32,8,128]{2,1,0:T(8,128)S(1)}, u32[]{:S(2)}, u32[]{:S(2)}) async-start(f32[32,8,128]{2,1,0:T(8,128)} %get-tuple-element.30), calls=%async_computation.2 | async-start | bytes 262144 | tf_op jit(solution)/shard_map/all_to_all | solution.py:968
  63.8 30.8 %copy-start = (bf16[32,16,16,128]{3,2,1,0:T(8,128)(2,1)S(1)}, bf16[32,16,16,128]{3,2,1,0:T(8,128)(2,1)}, u32[]{:S(2)}) copy-start(bf16[32,16,16,128]{3,2,1,0:T(8,128)(2,1)} %f_ref.1) | copy-start | bytes 6291460
  75.5 25.6 %copy-start.1 = (bf16[27,32]{1,0:T(8,128)(2,1)S(1)}, bf16[27,32]{1,0:T(8,128)(2,1)}, u32[]{:S(2)}) copy-start(bf16[27,32]{1,0:T(8,128)(2,1)} %w_ref.1) | copy-start | bytes 5188
  75.5 3.5 %collective-permute-start.2 = (f32[13,16,128]{2,1,0:T(8,128)S(1)}, f32[13,16,128]{2,1,0:T(8,128)S(1)}, u32[]{:S(2)}, u32[]{:S(2)}) collective-permute-start(f32[13,16,128]{2,1,0:T(8,128)S(1)} %get-tuple-element.35), channel_id=1, source_target_pairs={{0,8},{8,16},{16,24},{24,28},{28,20},{20,12},{12,4},{4,5},{5,13},{... | collective-permute-start | bytes 319496 | tf_op jit(solution)/shard_map/ppermute | solution.py:980
  77.7 4.3 %collective-permute-start.3 = (f32[13,16,128]{2,1,0:T(8,128)S(1)}, f32[13,16,128]{2,1,0:T(8,128)S(1)}, u32[]{:S(2)}, u32[]{:S(2)}) collective-permute-start(f32[13,16,128]{2,1,0:T(8,128)S(1)} %get-tuple-element.36), channel_id=1, source_target_pairs={{8,0},{16,8},{24,16},{28,24},{20,28},{12,20},{4,12},{5,4},{13,5},{... | collective-permute-start | bytes 319496 | tf_op jit(solution)/shard_map/ppermute | solution.py:980
  97.3 11.6 %all-to-all-start.4 = ((f32[32,8,128]{2,1,0:T(8,128)}), f32[32,8,128]{2,1,0:T(8,128)S(1)}, u32[]{:S(2)}, u32[]{:S(2)}) async-start(f32[32,8,128]{2,1,0:T(8,128)} %get-tuple-element.41.after_ref), calls=%async_computation.4 | async-start | bytes 262144 | tf_op jit(solution)/shard_map/all_to_all | solution.py:968

commit v3 on v2

--- a/solution.py
+++ b/solution.py
@@ -518,7 +518,7 @@
     rank = pos_ref[0]
     mask = masks(plan)
 
-    for ref in e_refs:
+    for ref in e_refs + g_refs:
         ref[...] = jnp.zeros_like(ref)
     zy_ref[...] = jnp.zeros_like(zy_ref)
     count_tables(plan, cross_ref, box_ref)
@@ -794,6 +794,13 @@
                 out_ref[a * plan.gy + b, q] = piece
 
 
+def fetch_kernel(plan, far_ref, after_ref, near_ref, sem_ref):
+    del plan, after_ref
+    copy = pltpu.make_async_copy(far_ref, near_ref, sem_ref.at[0])
+    copy.start()
+    copy.wait()
+
+
 def weight_kernel(
     plan, pos_ref, f_ref, bias_ref, got_ref, gw_ref, g_ref, dw_ref
 ):
@@ -945,7 +952,7 @@
     x, y, z = (lax.axis_index(axis).astype(jnp.int32) for axis in ALL_AXES)
     mine = y * plan.gx + jnp.where(y % 2 == 0, x, plan.gx - 1 - x)
     place = z * members + jnp.where(z % 2 == 0, mine, members - 1 - mine)
-    pos = pltpu.with_memory_space_constraint(jnp.stack([place, y]), pltpu.HBM)
+    pos = jnp.stack([place, y])
 
     def call(
         kernel, out_shape, in_specs, operands, micros, scratch=(), out_specs=None
@@ -979,8 +986,7 @@
         ]
         return lax.ppermute(array, ALL_AXES, pairs)
 
-    turned = pltpu.with_memory_space_constraint(weight.T, pltpu.HBM)
-    features_ahead = features
+    turned = weight.T
     features, weight, label = (
         pltpu.with_memory_space_constraint(a, pltpu.HBM) for a in (features, weight, label)
     )
@@ -1114,6 +1120,14 @@
         [pltpu.VMEM(span, f32), pltpu.VMEM((plan.span * tiles, LANES), f32)],
     )
 
+    features_ahead = call(
+        fetch_kernel,
+        pltpu.VMEM(features.shape, bf16),
+        [FAR, ANY],
+        (features, bias_part),
+        1,
+        [pltpu.SemaphoreType.DMA((1,))],
+    )
     moved = shape((plan.nx + 2, 3 * plan.Y, plan.nz), bf16)
     partial, g = call(
         weight_kernel,

time: 110 us -> 110 us (level)
  blocking collectives: 24.4 us -> 12.8 us
  starting transfers between devices: 25.2 us -> 31.9 us
  waiting for transfers between devices: 6.96 us -> 11.4 us
  Pallas kernels: 49.8 us -> 51.2 us
    all_to_all x2 -> x1, blocking collectives: 24.4 us -> 12.8 us  [exchange(): return lax.all_to_all(array, GROUP, 0, 0, tiled=True)]
    all_to_all x0 -> x1, starting transfers between devices: none -> 6.51 us  [exchange(): return lax.all_to_all(array, GROUP, 0, 0, tiled=True)]
    all_to_all x0 -> x1, waiting for transfers between devices: none -> 3.68 us  [exchange(): return lax.all_to_all(array, GROUP, 0, 0, tiled=True)]
    pallas_call x10 -> x11, Pallas kernels: 49.8 us -> 51.2 us  [call(): pl.pallas_call(functools.partial(kernel, plan), out_shape=out_shape, in_s...]
  transfers between devices with their start and end apart: 7 -> 8, of which waited for: 3 -> 4; matrix products, arithmetic and copies ran while one was open for 1% -> 1% of each run, Pallas kernels for 26% -> 27%
where the time goes in v3:
time: 110 us; the launch traced here: 109 us
  Pallas kernels  51.2 us (47%)
  starting transfers between devices  31.9 us (29%)
  blocking collectives  12.8 us (12%)
  waiting for transfers between devices  11.4 us (10%)
  between operations  1.45 us (1%)
    pallas_call x11, Pallas kernels, call(): pl.pallas_call(functools.partial(kernel, plan), out_shape=out_shape, in_s...  51.2 us
    all_to_all x3, starting transfers between devices, everywhere(): return lax.all_to_all(array, ALL_AXES, 0, 0, tiled=True)  18.6 us
    all_to_all x1, blocking collectives, exchange(): return lax.all_to_all(array, GROUP, 0, 0, tiled=True)  12.8 us
    ppermute x4, starting transfers between devices, hop(): return lax.ppermute(array, ALL_AXES, pairs)  6.83 us
    all_to_all x1, starting transfers between devices, exchange(): return lax.all_to_all(array, GROUP, 0, 0, tiled=True)  6.51 us
    ppermute x4, waiting for transfers between devices, hop(): return lax.ppermute(array, ALL_AXES, pairs)  4.55 us
    all_to_all x1, waiting for transfers between devices, exchange(): return lax.all_to_all(array, GROUP, 0, 0, tiled=True)  3.68 us
    all_to_all x3, waiting for transfers between devices, everywhere(): return lax.all_to_all(array, ALL_AXES, 0, 0, tiled=True)  3.17 us
  transfers between devices with their start and end apart: 8, of which 4 were waited for; matrix products, arithmetic and copies ran while one was open for 1% of the time, Pallas kernels for 27%

profile of v3, /device:TPU:0, one launch (start us, length us, event | category | flops | bytes accessed | tf_op | source)
XLA Modules:
  0.0 109.4 jit_solution(10908351691383197545)
XLA Ops:
  0.7 0.1 pad_add_fusion.pos_ref.refs_0_
  0.7 3.6 %shard_map.75 = f32[8,6,16,128]{3,2,1,0:T(8,128)S(1)} custom-call(s32[2]{0:T(128)S(1)} %pad_add_fusion.pos_ref.refs_0_, bf16[27,32]{1,0:T(8,128)(2,1)} %w_ref.1, bf16[32,16,16,128]{3,2,1,0:T(8,128)(2,1)} %far_ref.3, s32[16,16,128]{2,1,0:T(8,128)} %label_ref.1), custom_call_target="tpu_custom_call" | custom-call | bytes 175000 | tf_op jit(solution)/shard_map/pallas_call | solution.py:962
  4.3 12.8 %all_to_all.25.got_ref = f32[8,6,16,128]{3,2,1,0:T(8,128)S(1)} all-to-all(f32[8,6,16,128]{3,2,1,0:T(8,128)S(1)} %shard_map.75), channel_id=1, replica_groups=mesh['gx'=4,'gy'=2,'gz'=4] {'gx','gy'}, dimensions={0} | all-to-all | bytes 786432 | tf_op jit(solution)/shard_map/all_to_all | solution.py:972
  17.1 0.2 shard_map.76
  17.3 2.1 %collective-permute-start = (f32[21,16,128]{2,1,0:T(8,128)S(1)}, f32[21,16,128]{2,1,0:T(8,128)S(1)}, u32[]{:S(2)}, u32[]{:S(2)}) collective-permute-start(f32[21,16,128]{2,1,0:T(8,128)S(1)} %bitcast.15), channel_id=1, source_target_pairs={{0,8},{8,16},{16,24},{24,28},{28,20},{20,12},{12,4},{4,5},{5,13},{... | collective-permute-start | bytes 516104 | tf_op jit(solution)/shard_map/ppermute | solution.py:987
  19.4 1.3 %collective-permute-start.1 = (f32[21,16,128]{2,1,0:T(8,128)S(1)}, f32[21,16,128]{2,1,0:T(8,128)S(1)}, u32[]{:S(2)}, u32[]{:S(2)}) collective-permute-start(f32[21,16,128]{2,1,0:T(8,128)S(1)} %bitcast.14), channel_id=1, source_target_pairs={{8,0},{16,8},{24,16},{28,24},{20,28},{12,20},{4,12},{5,4},{13,5},{... | collective-permute-start | bytes 516104 | tf_op jit(solution)/shard_map/ppermute | solution.py:987
  21.4 0.0 collective-permute-done.refs_4_.refs_3_
  21.4 1.5 %collective-permute-done.1.refs_5_.refs_4_ = f32[21,16,128]{2,1,0:T(8,128)S(1)} collective-permute-done((f32[21,16,128]{2,1,0:T(8,128)S(1)}, f32[21,16,128]{2,1,0:T(8,128)S(1)}, u32[]{:S(2)}, u32[]{:S(2)}) %collective-permute-start.1) | collective-permute-done | bytes 172064 | tf_op jit(solution)/shard_map/ppermute | solution.py:987
  22.9 13.2 %shard_map.77 = (f32[11,66,16,128]{3,2,1,0:T(8,128)}, f32[18,16,128]{2,1,0:T(8,128)S(1)}, f32[32,8,128]{2,1,0:T(8,128)}) custom-call(s32[2]{0:T(128)S(1)} %pad_add_fusion.pos_ref.refs_0_, f32[1]{0:T(128)S(6)} %copy.9.refs_1_, f32[16,16,128]{2,1,0:T(8,128)S(1)} %bitcast.9, f32[26,16,128]{2,1,0:T(8,128)S(1)} %bitcast.12, ...), custom_call_target="tpu_custom_call" | custom-call | bytes 275000 | tf_op jit(solution)/shard_map/pallas_call | solution.py:962
  36.1 8.7 %all-to-all-start.1 = ((f32[32,8,128]{2,1,0:T(8,128)}), f32[32,8,128]{2,1,0:T(8,128)S(1)}, u32[]{:S(2)}, u32[]{:S(2)}) async-start(f32[32,8,128]{2,1,0:T(8,128)} %get-tuple-element.28), calls=%async_computation.1 | async-start | bytes 262144 | tf_op jit(solution)/shard_map/all_to_all | solution.py:975
  44.8 12.3 %shard_map.78 = (f32[18,16,128]{2,1,0:T(8,128)S(1)}, f32[18,16,128]{2,1,0:T(8,128)S(1)}, f32[32,8,128]{2,1,0:T(8,128)}) custom-call(s32[2]{0:T(128)S(1)} %pad_add_fusion.pos_ref.refs_0_, f32[18,16,128]{2,1,0:T(8,128)S(1)} %get-tuple-element.29.refs_1_.refs_3_, f32[16,16,128]{2,1,0:T(8,128)S(1)} %bitcast.10, ...), custom_call_target="tpu_custom_call" | custom-call | bytes 325000 | tf_op jit(solution)/shard_map/pallas_call | solution.py:962
  57.1 0.0 all-to-all-done.1.refs_1_
  57.1 5.8 %all-to-all-start.2 = ((f32[32,8,128]{2,1,0:T(8,128)}), f32[32,8,128]{2,1,0:T(8,128)S(1)}, u32[]{:S(2)}, u32[]{:S(2)}) async-start(f32[32,8,128]{2,1,0:T(8,128)} %get-tuple-element.30), calls=%async_computation.2 | async-start | bytes 262144 | tf_op jit(solution)/shard_map/all_to_all | solution.py:975
  63.0 11.4 %shard_map.79 = (f32[18,16,128]{2,1,0:T(8,128)S(1)}, f32[13,16,128]{2,1,0:T(8,128)S(1)}, f32[13,16,128]{2,1,0:T(8,128)S(1)}) custom-call(s32[2]{0:T(128)S(1)} %pad_add_fusion.pos_ref.refs_0_, f32[32,8,128]{2,1,0:T(8,128)S(1)} %all-to-all-done.1.refs_1_, f32[16,16,128]{2,1,0:T(8,128)S(1)} %bitcast.11, f32[11,66,16,128]{3,2,1,0:T(8,128)} %get-tuple-element.33.refs_3_), custom_call_target="tpu_custom_call" | custom-call | bytes 275000 | tf_op jit(solution)/shard_map/pallas_call | solution.py:962
  74.4 2.2 %collective-permute-start.2 = (f32[13,16,128]{2,1,0:T(8,128)S(1)}, f32[13,16,128]{2,1,0:T(8,128)S(1)}, u32[]{:S(2)}, u32[]{:S(2)}) collective-permute-start(f32[13,16,128]{2,1,0:T(8,128)S(1)} %get-tuple-element.35), channel_id=1, source_target_pairs={{0,8},{8,16},{16,24},{24,28},{28,20},{20,12},{12,4},{4,5},{5,13},{... | collective-permute-start | bytes 319496 | tf_op jit(solution)/shard_map/ppermute | solution.py:987
  76.6 1.3 %collective-permute-start.3 = (f32[13,16,128]{2,1,0:T(8,128)S(1)}, f32[13,16,128]{2,1,0:T(8,128)S(1)}, u32[]{:S(2)}, u32[]{:S(2)}) collective-permute-start(f32[13,16,128]{2,1,0:T(8,128)S(1)} %get-tuple-element.36), channel_id=1, source_target_pairs={{8,0},{16,8},{24,16},{28,24},{20,28},{12,20},{4,12},{5,4},{13,5},{... | collective-permute-start | bytes 319496 | tf_op jit(solution)/shard_map/ppermute | solution.py:987
  77.9 0.0 all-to-all-done.2.refs_2_
  77.9 0.0 collective-permute-done.2.refs_7_
  77.9 3.0 %collective-permute-done.3.refs_8_ = f32[13,16,128]{2,1,0:T(8,128)S(1)} collective-permute-done((f32[13,16,128]{2,1,0:T(8,128)S(1)}, f32[13,16,128]{2,1,0:T(8,128)S(1)}, u32[]{:S(2)}, u32[]{:S(2)}) %collective-permute-start.3) | collective-permute-done | bytes 106528 | tf_op jit(solution)/shard_map/ppermute | solution.py:987
  80.9 1.5 %shard_map.80 = (bf16[8,6,16,128]{3,2,1,0:T(8,128)(2,1)}, f32[8,128]{1,0:T(8,128)S(1)}, f32[8,128]{1,0:T(8,128)S(1)}) custom-call(s32[2]{0:T(128)S(1)} %pad_add_fusion.pos_ref.refs_0_, f32[32,8,128]{2,1,0:T(8,128)S(1)} %all-to-all-done.1.refs_1_, f32[32,8,128]{2,1,0:T(8,128)S(1)} %all-to-all-done.2.refs_2_, ...), custom_call_target="tpu_custom_call" | custom-call | bytes 50000 | tf_op jit(solution)/shard_map/pallas_call | solution.py:962
  82.4 6.5 %all-to-all-start.3 = ((bf16[8,6,16,128]{3,2,1,0:T(8,128)(2,1)}), bf16[8,6,16,128]{3,2,1,0:T(8,128)(2,1)S(1)}, u32[]{:S(2)}, u32[]{:S(2)}) async-start(bf16[8,6,16,128]{3,2,1,0:T(8,128)(2,1)} %get-tuple-element.39), calls=%async_computation.3 | async-start | bytes 393216 | tf_op jit(solution)/shard_map/all_to_all | solution.py:972
  88.9 1.6 %shard_map.82.f_ref = bf16[32,16,16,128]{3,2,1,0:T(8,128)(2,1)S(1)} custom-call(bf16[32,16,16,128]{3,2,1,0:T(8,128)(2,1)} %far_ref.3, f32[8,128]{1,0:T(8,128)S(1)} %get-tuple-element.38.after_ref.bias_ref), custom_call_target="tpu_custom_call" | custom-call | bytes 25000 | tf_op jit(solution)/shard_map/pallas_call | solution.py:962
  90.5 0.0 copy-start
  90.5 3.7 %all-to-all-done.3.got_ref = bf16[8,6,16,128]{3,2,1,0:T(8,128)(2,1)S(1)} async-done(((bf16[8,6,16,128]{3,2,1,0:T(8,128)(2,1)}), bf16[8,6,16,128]{3,2,1,0:T(8,128)(2,1)S(1)}, u32[]{:S(2)}, u32[]{:S(2)}) %all-to-all-start.3) | async-done | bytes 196640 | tf_op jit(solution)/shard_map/all_to_all | solution.py:972
  94.2 2.6 %shard_map.83 = (f32[32,8,128]{2,1,0:T(8,128)}, bf16[18,96,128]{2,1,0:T(8,128)(2,1)S(1)}) custom-call(s32[2]{0:T(128)S(1)} %pad_add_fusion.pos_ref.refs_0_, bf16[32,16,16,128]{3,2,1,0:T(8,128)(2,1)S(1)} %shard_map.82.f_ref, f32[8,128]{1,0:T(8,128)S(1)} %get-tuple-element.38.after_ref.bias_ref, bf16[8,6,16,128]{3,2,1,0:T(8,128)(2,1)S(1)} %all-to-all-done.3.got_ref), custom_call_target="tpu_custom_call" | custom-call | bytes 125000 | tf_op jit(solution)/shard_map/pallas_call | solution.py:962
  96.9 4.1 %all-to-all-start.4 = ((f32[32,8,128]{2,1,0:T(8,128)}), f32[32,8,128]{2,1,0:T(8,128)S(1)}, u32[]{:S(2)}, u32[]{:S(2)}) async-start(f32[32,8,128]{2,1,0:T(8,128)} %get-tuple-element.41.after_ref), calls=%async_computation.4 | async-start | bytes 262144 | tf_op jit(solution)/shard_map/all_to_all | solution.py:975
  100.9 0.0 copy-done
  100.9 0.1 copy.8
  101.0 1.4 %shard_map.81.wide_ref = bf16[512,288]{1,0:T(8,128)(2,1)S(1)} custom-call(s32[2]{0:T(128)S(1)} %pad_add_fusion.pos_ref.refs_0_, bf16[32,27]{1,0:T(8,128)(2,1)S(1)} %bitcast.13, f32[18,16,128]{2,1,0:T(8,128)S(1)} %get-tuple-element.34.refs_6_.after_ref), custom_call_target="tpu_custom_call" | custom-call | bytes 50000 | tf_op jit(solution)/shard_map/pallas_call | solution.py:962
  102.5 0.5 slice.3
  103.0 2.6 %shard_map.84 = bf16[32,16,16,128]{3,2,1,0:T(8,128)(2,1)} custom-call(bf16[512,288]{1,0:T(8,128)(2,1)S(1)} %shard_map.81.wide_ref, bf16[18,96,128]{2,1,0:T(8,128)(2,1)S(1)} %get-tuple-element.40.g_ref, f32[32,8,128]{2,1,0:T(8,128)} %get-tuple-element.41.after_ref), custom_call_target="tpu_custom_call" | custom-call | bytes 125000 | tf_op jit(solution)/shard_map/pallas_call | solution.py:962
  105.6 3.2 %all-to-all-done.4.got_ref = f32[32,8,128]{2,1,0:T(8,128)S(1)} async-done(((f32[32,8,128]{2,1,0:T(8,128)}), f32[32,8,128]{2,1,0:T(8,128)S(1)}, u32[]{:S(2)}, u32[]{:S(2)}) %all-to-all-start.4) | async-done | bytes 131104 | tf_op jit(solution)/shard_map/all_to_all | solution.py:975
  108.7 0.7 shard_map.85
Async XLA Ops:
  17.3 4.0 %collective-permute-start = (f32[21,16,128]{2,1,0:T(8,128)S(1)}, f32[21,16,128]{2,1,0:T(8,128)S(1)}, u32[]{:S(2)}, u32[]{:S(2)}) collective-permute-start(f32[21,16,128]{2,1,0:T(8,128)S(1)} %bitcast.15), channel_id=1, source_target_pairs={{0,8},{8,16},{16,24},{24,28},{28,20},{20,12},{12,4},{4,5},{5,13},{... | collective-permute-start | bytes 516104 | tf_op jit(solution)/shard_map/ppermute | solution.py:987
  19.4 3.5 %collective-permute-start.1 = (f32[21,16,128]{2,1,0:T(8,128)S(1)}, f32[21,16,128]{2,1,0:T(8,128)S(1)}, u32[]{:S(2)}, u32[]{:S(2)}) collective-permute-start(f32[21,16,128]{2,1,0:T(8,128)S(1)} %bitcast.14), channel_id=1, source_target_pairs={{8,0},{16,8},{24,16},{28,24},{20,28},{12,20},{4,12},{5,4},{13,5},{... | collective-permute-start | bytes 516104 | tf_op jit(solution)/shard_map/ppermute | solution.py:987
  36.1 21.0 %all-to-all-start.1 = ((f32[32,8,128]{2,1,0:T(8,128)}), f32[32,8,128]{2,1,0:T(8,128)S(1)}, u32[]{:S(2)}, u32[]{:S(2)}) async-start(f32[32,8,128]{2,1,0:T(8,128)} %get-tuple-element.28), calls=%async_computation.1 | async-start | bytes 262144 | tf_op jit(solution)/shard_map/all_to_all | solution.py:975
  57.1 20.8 %all-to-all-start.2 = ((f32[32,8,128]{2,1,0:T(8,128)}), f32[32,8,128]{2,1,0:T(8,128)S(1)}, u32[]{:S(2)}, u32[]{:S(2)}) async-start(f32[32,8,128]{2,1,0:T(8,128)} %get-tuple-element.30), calls=%async_computation.2 | async-start | bytes 262144 | tf_op jit(solution)/shard_map/all_to_all | solution.py:975
  74.4 3.5 %collective-permute-start.2 = (f32[13,16,128]{2,1,0:T(8,128)S(1)}, f32[13,16,128]{2,1,0:T(8,128)S(1)}, u32[]{:S(2)}, u32[]{:S(2)}) collective-permute-start(f32[13,16,128]{2,1,0:T(8,128)S(1)} %get-tuple-element.35), channel_id=1, source_target_pairs={{0,8},{8,16},{16,24},{24,28},{28,20},{20,12},{12,4},{4,5},{5,13},{... | collective-permute-start | bytes 319496 | tf_op jit(solution)/shard_map/ppermute | solution.py:987
  76.6 4.3 %collective-permute-start.3 = (f32[13,16,128]{2,1,0:T(8,128)S(1)}, f32[13,16,128]{2,1,0:T(8,128)S(1)}, u32[]{:S(2)}, u32[]{:S(2)}) collective-permute-start(f32[13,16,128]{2,1,0:T(8,128)S(1)} %get-tuple-element.36), channel_id=1, source_target_pairs={{8,0},{16,8},{24,16},{28,24},{20,28},{12,20},{4,12},{5,4},{13,5},{... | collective-permute-start | bytes 319496 | tf_op jit(solution)/shard_map/ppermute | solution.py:987
  82.4 11.8 %all-to-all-start.3 = ((bf16[8,6,16,128]{3,2,1,0:T(8,128)(2,1)}), bf16[8,6,16,128]{3,2,1,0:T(8,128)(2,1)S(1)}, u32[]{:S(2)}, u32[]{:S(2)}) async-start(bf16[8,6,16,128]{3,2,1,0:T(8,128)(2,1)} %get-tuple-element.39), calls=%async_computation.3 | async-start | bytes 393216 | tf_op jit(solution)/shard_map/all_to_all | solution.py:972
  90.5 10.4 %copy-start = (bf16[27,32]{1,0:T(8,128)(2,1)S(1)}, bf16[27,32]{1,0:T(8,128)(2,1)}, u32[]{:S(2)}) copy-start(bf16[27,32]{1,0:T(8,128)(2,1)} %w_ref.1) | copy-start | bytes 5188
  96.9 11.9 %all-to-all-start.4 = ((f32[32,8,128]{2,1,0:T(8,128)}), f32[32,8,128]{2,1,0:T(8,128)S(1)}, u32[]{:S(2)}, u32[]{:S(2)}) async-start(f32[32,8,128]{2,1,0:T(8,128)} %get-tuple-element.41.after_ref), calls=%async_computation.4 | async-start | bytes 262144 | tf_op jit(solution)/shard_map/all_to_all | solution.py:975

commit v4 on v3

--- a/solution.py
+++ b/solution.py
@@ -493,14 +493,20 @@
 
 
 def put_sums(plan, ref, totals):
-    lines = [jnp.sum(total, axis=0, keepdims=True) for total in totals]
-    lines += [jnp.zeros((1, LANES), f32)] * (8 - len(lines))
-    ref[...] = jnp.broadcast_to(jnp.concatenate(lines, axis=0)[None], (plan.ranks, 8, LANES))
+    lane = lane_iota((1, LANES))
+    line = jnp.zeros((1, LANES), f32)
+    for n, total in enumerate(totals):
+        whole = jnp.sum(jnp.sum(total, axis=0, keepdims=True), axis=1, keepdims=True)
+        line = jnp.where(lane == n, whole, line)
+    ref[...] = jnp.broadcast_to(line[None], (plan.ranks, 1, LANES))
 
 
 def get_sums(ref, count):
-    lines = jnp.sum(jnp.sum(ref[...], axis=0), axis=1, keepdims=True)
-    return [lines[n : n + 1] for n in range(count)]
+    line = jnp.sum(ref[...], axis=0)
+    lane = lane_iota((1, LANES))
+    return [
+        jnp.sum(jnp.where(lane == n, line, 0.0), axis=1, keepdims=True) for n in range(count)
+    ]
 
 
 def forward_kernel(plan, *refs):
@@ -1030,7 +1036,7 @@
 
     slab = (zc, tiles, LANES)
     span = (plan.span, tiles, LANES)
-    everyone = shape((plan.ranks, 8, LANES))
+    everyone = shape((plan.ranks, 1, LANES))
     table = pltpu.VMEM((3, tiles, LANES), f32)
 
     records = pltpu.HBM((SECTIONS, plan.records, tiles, LANES), f32)

time: 110 us -> 112 us (1.018)
  blocking collectives: 12.8 us -> 39.2 us
  starting transfers between devices: 31.9 us -> 12.4 us
  waiting for transfers between devices: 11.4 us -> 8.3 us
  Pallas kernels: 51.2 us -> 49.9 us
    all_to_all x0 -> x2, blocking collectives: none -> 26.4 us  [everywhere(): return lax.all_to_all(array, ALL_AXES, 0, 0, tiled=True)]
    all_to_all x3 -> x1, starting transfers between devices: 18.6 us -> 2.56 us  [everywhere(): return lax.all_to_all(array, ALL_AXES, 0, 0, tiled=True)]
    all_to_all x1, starting transfers between devices: 6.51 us -> 3.39 us  [exchange(): return lax.all_to_all(array, GROUP, 0, 0, tiled=True)]
    ppermute x4, waiting for transfers between devices: 4.55 us -> 1.53 us  [hop(): return lax.ppermute(array, ALL_AXES, pairs)]
    pallas_call x11, Pallas kernels: 51.2 us -> 49.9 us  [call(): pl.pallas_call(functools.partial(kernel, plan), out_shape=out_shape, in_s...]
    all_to_all x3 -> x1, waiting for transfers between devices: 3.17 us -> 3.17 us  [everywhere(): return lax.all_to_all(array, ALL_AXES, 0, 0, tiled=True)]
  transfers between devices with their start and end apart: 8 -> 6, of which waited for: 4 -> 3; matrix products, arithmetic and copies ran while one was open for 1% -> 1% of each run, Pallas kernels for 27% -> 15%
where the time goes in v4:
time: 112 us
  Pallas kernels  49.9 us (45%)
  blocking collectives  39.2 us (35%)
  starting transfers between devices  12.4 us (11%)
  waiting for transfers between devices  8.3 us (7%)
  between operations  1.43 us (1%)
    pallas_call x11, Pallas kernels, call(): pl.pallas_call(functools.partial(kernel, plan), out_shape=out_shape, in_s...  49.9 us
    all_to_all x2, blocking collectives, everywhere(): return lax.all_to_all(array, ALL_AXES, 0, 0, tiled=True)  26.4 us
    all_to_all x1, blocking collectives, exchange(): return lax.all_to_all(array, GROUP, 0, 0, tiled=True)  12.8 us
    ppermute x4, starting transfers between devices, hop(): return lax.ppermute(array, ALL_AXES, pairs)  6.42 us
    all_to_all x1, waiting for transfers between devices, exchange(): return lax.all_to_all(array, GROUP, 0, 0, tiled=True)  3.61 us
    all_to_all x1, starting transfers between devices, exchange(): return lax.all_to_all(array, GROUP, 0, 0, tiled=True)  3.39 us
    all_to_all x1, waiting for transfers between devices, everywhere(): return lax.all_to_all(array, ALL_AXES, 0, 0, tiled=True)  3.17 us
    all_to_all x1, starting transfers between devices, everywhere(): return lax.all_to_all(array, ALL_AXES, 0, 0, tiled=True)  2.56 us
  transfers between devices with their start and end apart: 6, of which 3 were waited for; matrix products, arithmetic and copies ran while one was open for 1% of the time, Pallas kernels for 15%

profile of v4, /device:TPU:0, one launch (start us, length us, event | category | flops | bytes accessed | tf_op | source)
XLA Modules:
  0.0 111.9 jit_solution(6535765231415740078)
XLA Ops:
  0.7 0.1 pad_add_fusion.pos_ref.refs_0_
  0.7 3.6 %shard_map.75 = f32[8,6,16,128]{3,2,1,0:T(8,128)S(1)} custom-call(s32[2]{0:T(128)S(1)} %pad_add_fusion.pos_ref.refs_0_, bf16[27,32]{1,0:T(8,128)(2,1)} %w_ref.1, bf16[32,16,16,128]{3,2,1,0:T(8,128)(2,1)} %far_ref.3, s32[16,16,128]{2,1,0:T(8,128)} %label_ref.1), custom_call_target="tpu_custom_call" | custom-call | bytes 175000 | tf_op jit(solution)/shard_map/pallas_call | solution.py:968
  4.3 12.8 %all_to_all.25.got_ref = f32[8,6,16,128]{3,2,1,0:T(8,128)S(1)} all-to-all(f32[8,6,16,128]{3,2,1,0:T(8,128)S(1)} %shard_map.75), channel_id=1, replica_groups=mesh['gx'=4,'gy'=2,'gz'=4] {'gx','gy'}, dimensions={0} | all-to-all | bytes 786432 | tf_op jit(solution)/shard_map/all_to_all | solution.py:978
  17.1 0.2 shard_map.76
  17.3 2.1 %collective-permute-start = (f32[21,16,128]{2,1,0:T(8,128)S(1)}, f32[21,16,128]{2,1,0:T(8,128)S(1)}, u32[]{:S(2)}, u32[]{:S(2)}) collective-permute-start(f32[21,16,128]{2,1,0:T(8,128)S(1)} %bitcast.15), channel_id=1, source_target_pairs={{0,8},{8,16},{16,24},{24,28},{28,20},{20,12},{12,4},{4,5},{5,13},{... | collective-permute-start | bytes 516104 | tf_op jit(solution)/shard_map/ppermute | solution.py:993
  19.4 1.3 %collective-permute-start.1 = (f32[21,16,128]{2,1,0:T(8,128)S(1)}, f32[21,16,128]{2,1,0:T(8,128)S(1)}, u32[]{:S(2)}, u32[]{:S(2)}) collective-permute-start(f32[21,16,128]{2,1,0:T(8,128)S(1)} %bitcast.14), channel_id=1, source_target_pairs={{8,0},{16,8},{24,16},{28,24},{20,28},{12,20},{4,12},{5,4},{13,5},{... | collective-permute-start | bytes 516104 | tf_op jit(solution)/shard_map/ppermute | solution.py:993
  21.4 0.0 collective-permute-done.refs_4_.refs_3_
  21.4 1.5 %collective-permute-done.1.refs_5_.refs_4_ = f32[21,16,128]{2,1,0:T(8,128)S(1)} collective-permute-done((f32[21,16,128]{2,1,0:T(8,128)S(1)}, f32[21,16,128]{2,1,0:T(8,128)S(1)}, u32[]{:S(2)}, u32[]{:S(2)}) %collective-permute-start.1) | collective-permute-done | bytes 172064 | tf_op jit(solution)/shard_map/ppermute | solution.py:993
  22.9 12.6 %shard_map.77 = (f32[11,66,16,128]{3,2,1,0:T(8,128)}, f32[18,16,128]{2,1,0:T(8,128)S(1)}, f32[32,1,128]{2,1,0:T(1,128)S(1)}) custom-call(s32[2]{0:T(128)S(1)} %pad_add_fusion.pos_ref.refs_0_, f32[1]{0:T(128)S(6)} %copy.9.refs_1_, f32[16,16,128]{2,1,0:T(8,128)S(1)} %bitcast.9, f32[26,16,128]{2,1,0:T(8,128)S(1)} %bitcast.12, ...), custom_call_target="tpu_custom_call" | custom-call | bytes 275000 | tf_op jit(solution)/shard_map/pallas_call | solution.py:968
  35.5 15.7 %all_to_all.26.refs_1_ = f32[32,1,128]{2,1,0:T(1,128)S(1)} all-to-all(f32[32,1,128]{2,1,0:T(1,128)S(1)} %get-tuple-element.28), channel_id=1, replica_groups=mesh['gx'=4,'gy'=2,'gz'=4] {'gx','gy','gz'}, dimensions={0} | all-to-all | bytes 32768 | tf_op jit(solution)/shard_map/all_to_all | solution.py:981
  51.1 11.4 %shard_map.79 = (f32[18,16,128]{2,1,0:T(8,128)S(1)}, f32[13,16,128]{2,1,0:T(8,128)S(1)}, f32[13,16,128]{2,1,0:T(8,128)S(1)}) custom-call(s32[2]{0:T(128)S(1)} %pad_add_fusion.pos_ref.refs_0_, f32[32,1,128]{2,1,0:T(1,128)S(1)} %all_to_all.26.refs_1_, f32[16,16,128]{2,1,0:T(8,128)S(1)} %bitcast.10, f32[11,66,16,128]{3,2,1,0:T(8,128)} %get-tuple-element.33.refs_3_), custom_call_target="tpu_custom_call" | custom-call | bytes 275000 | tf_op jit(solution)/shard_map/pallas_call | solution.py:968
  62.6 1.7 %collective-permute-start.2 = (f32[13,16,128]{2,1,0:T(8,128)S(1)}, f32[13,16,128]{2,1,0:T(8,128)S(1)}, u32[]{:S(2)}, u32[]{:S(2)}) collective-permute-start(f32[13,16,128]{2,1,0:T(8,128)S(1)} %get-tuple-element.35), channel_id=1, source_target_pairs={{0,8},{8,16},{16,24},{24,28},{28,20},{20,12},{12,4},{4,5},{5,13},{... | collective-permute-start | bytes 319496 | tf_op jit(solution)/shard_map/ppermute | solution.py:993
  64.3 1.3 %collective-permute-start.3 = (f32[13,16,128]{2,1,0:T(8,128)S(1)}, f32[13,16,128]{2,1,0:T(8,128)S(1)}, u32[]{:S(2)}, u32[]{:S(2)}) collective-permute-start(f32[13,16,128]{2,1,0:T(8,128)S(1)} %get-tuple-element.36), channel_id=1, source_target_pairs={{8,0},{16,8},{24,16},{28,24},{20,28},{12,20},{4,12},{5,4},{13,5},{... | collective-permute-start | bytes 319496 | tf_op jit(solution)/shard_map/ppermute | solution.py:993
  65.6 11.7 %shard_map.78 = (f32[18,16,128]{2,1,0:T(8,128)S(1)}, f32[18,16,128]{2,1,0:T(8,128)S(1)}, f32[32,1,128]{2,1,0:T(1,128)S(1)}) custom-call(s32[2]{0:T(128)S(1)} %pad_add_fusion.pos_ref.refs_0_, f32[18,16,128]{2,1,0:T(8,128)S(1)} %get-tuple-element.29.refs_1_.refs_3_, f32[16,16,128]{2,1,0:T(8,128)S(1)} %bitcast.11, ...), custom_call_target="tpu_custom_call" | custom-call | bytes 325000 | tf_op jit(solution)/shard_map/pallas_call | solution.py:968
  77.3 10.8 %all_to_all.27.refs_2_ = f32[32,1,128]{2,1,0:T(1,128)S(1)} all-to-all(f32[32,1,128]{2,1,0:T(1,128)S(1)} %get-tuple-element.30), channel_id=1, replica_groups=mesh['gx'=4,'gy'=2,'gz'=4] {'gx','gy','gz'}, dimensions={0} | all-to-all | bytes 32768 | tf_op jit(solution)/shard_map/all_to_all | solution.py:981
  88.1 0.0 collective-permute-done.2.refs_7_
  88.1 0.0 collective-permute-done.3.refs_8_
  88.1 1.5 %shard_map.80 = (bf16[8,6,16,128]{3,2,1,0:T(8,128)(2,1)}, f32[8,128]{1,0:T(8,128)S(1)}, f32[8,128]{1,0:T(8,128)S(1)}) custom-call(s32[2]{0:T(128)S(1)} %pad_add_fusion.pos_ref.refs_0_, f32[32,1,128]{2,1,0:T(1,128)S(1)} %all_to_all.26.refs_1_, f32[32,1,128]{2,1,0:T(1,128)S(1)} %all_to_all.27.refs_2_, f32[18,16,128]{2,1,0:T(8,128)S(1)} %get-tuple-element.29.refs_1_.refs_3_, ...), custom_call_target="tpu_custom_call" | custom-call | bytes 50000 | tf_op jit(solution)/shard_map/pallas_call | solution.py:968
  89.6 3.4 %all-to-all-start.3 = ((bf16[8,6,16,128]{3,2,1,0:T(8,128)(2,1)}), bf16[8,6,16,128]{3,2,1,0:T(8,128)(2,1)S(1)}, u32[]{:S(2)}, u32[]{:S(2)}) async-start(bf16[8,6,16,128]{3,2,1,0:T(8,128)(2,1)} %get-tuple-element.39), calls=%async_computation.3 | async-start | bytes 393216 | tf_op jit(solution)/shard_map/all_to_all | solution.py:978
  93.0 1.6 %shard_map.82.f_ref = bf16[32,16,16,128]{3,2,1,0:T(8,128)(2,1)S(1)} custom-call(bf16[32,16,16,128]{3,2,1,0:T(8,128)(2,1)} %far_ref.3, f32[8,128]{1,0:T(8,128)S(1)} %get-tuple-element.38.after_ref.bias_ref), custom_call_target="tpu_custom_call" | custom-call | bytes 25000 | tf_op jit(solution)/shard_map/pallas_call | solution.py:968
  94.6 0.0 copy-start
  94.6 3.6 %all-to-all-done.3.got_ref = bf16[8,6,16,128]{3,2,1,0:T(8,128)(2,1)S(1)} async-done(((bf16[8,6,16,128]{3,2,1,0:T(8,128)(2,1)}), bf16[8,6,16,128]{3,2,1,0:T(8,128)(2,1)S(1)}, u32[]{:S(2)}, u32[]{:S(2)}) %all-to-all-start.3) | async-done | bytes 196640 | tf_op jit(solution)/shard_map/all_to_all | solution.py:978
  98.2 2.6 %shard_map.83 = (f32[32,8,128]{2,1,0:T(8,128)}, bf16[18,96,128]{2,1,0:T(8,128)(2,1)S(1)}) custom-call(s32[2]{0:T(128)S(1)} %pad_add_fusion.pos_ref.refs_0_, bf16[32,16,16,128]{3,2,1,0:T(8,128)(2,1)S(1)} %shard_map.82.f_ref, f32[8,128]{1,0:T(8,128)S(1)} %get-tuple-element.38.after_ref.bias_ref, bf16[8,6,16,128]{3,2,1,0:T(8,128)(2,1)S(1)} %all-to-all-done.3.got_ref), custom_call_target="tpu_custom_call" | custom-call | bytes 125000 | tf_op jit(solution)/shard_map/pallas_call | solution.py:968
  100.8 2.6 %all-to-all-start.4 = ((f32[32,8,128]{2,1,0:T(8,128)}), f32[32,8,128]{2,1,0:T(8,128)S(1)}, u32[]{:S(2)}, u32[]{:S(2)}) async-start(f32[32,8,128]{2,1,0:T(8,128)} %get-tuple-element.41.after_ref), calls=%async_computation.4 | async-start | bytes 262144 | tf_op jit(solution)/shard_map/all_to_all | solution.py:981
  103.4 0.0 copy-done
  103.4 0.1 copy.8
  103.5 1.4 %shard_map.81.wide_ref = bf16[512,288]{1,0:T(8,128)(2,1)S(1)} custom-call(s32[2]{0:T(128)S(1)} %pad_add_fusion.pos_ref.refs_0_, bf16[32,27]{1,0:T(8,128)(2,1)S(1)} %bitcast.13, f32[18,16,128]{2,1,0:T(8,128)S(1)} %get-tuple-element.34.refs_6_.after_ref), custom_call_target="tpu_custom_call" | custom-call | bytes 50000 | tf_op jit(solution)/shard_map/pallas_call | solution.py:968
  104.9 0.5 slice.3
  105.4 2.6 %shard_map.84 = bf16[32,16,16,128]{3,2,1,0:T(8,128)(2,1)} custom-call(bf16[512,288]{1,0:T(8,128)(2,1)S(1)} %shard_map.81.wide_ref, bf16[18,96,128]{2,1,0:T(8,128)(2,1)S(1)} %get-tuple-element.40.g_ref, f32[32,8,128]{2,1,0:T(8,128)} %get-tuple-element.41.after_ref), custom_call_target="tpu_custom_call" | custom-call | bytes 125000 | tf_op jit(solution)/shard_map/pallas_call | solution.py:968
  108.0 3.2 %all-to-all-done.4.got_ref = f32[32,8,128]{2,1,0:T(8,128)S(1)} async-done(((f32[32,8,128]{2,1,0:T(8,128)}), f32[32,8,128]{2,1,0:T(8,128)S(1)}, u32[]{:S(2)}, u32[]{:S(2)}) %all-to-all-start.4) | async-done | bytes 131104 | tf_op jit(solution)/shard_map/all_to_all | solution.py:981
  111.2 0.7 shard_map.85
Async XLA Ops:
  17.3 4.0 %collective-permute-start = (f32[21,16,128]{2,1,0:T(8,128)S(1)}, f32[21,16,128]{2,1,0:T(8,128)S(1)}, u32[]{:S(2)}, u32[]{:S(2)}) collective-permute-start(f32[21,16,128]{2,1,0:T(8,128)S(1)} %bitcast.15), channel_id=1, source_target_pairs={{0,8},{8,16},{16,24},{24,28},{28,20},{20,12},{12,4},{4,5},{5,13},{... | collective-permute-start | bytes 516104 | tf_op jit(solution)/shard_map/ppermute | solution.py:993
  19.4 3.5 %collective-permute-start.1 = (f32[21,16,128]{2,1,0:T(8,128)S(1)}, f32[21,16,128]{2,1,0:T(8,128)S(1)}, u32[]{:S(2)}, u32[]{:S(2)}) collective-permute-start(f32[21,16,128]{2,1,0:T(8,128)S(1)} %bitcast.14), channel_id=1, source_target_pairs={{8,0},{16,8},{24,16},{28,24},{20,28},{12,20},{4,12},{5,4},{13,5},{... | collective-permute-start | bytes 516104 | tf_op jit(solution)/shard_map/ppermute | solution.py:993
  62.6 25.5 %collective-permute-start.2 = (f32[13,16,128]{2,1,0:T(8,128)S(1)}, f32[13,16,128]{2,1,0:T(8,128)S(1)}, u32[]{:S(2)}, u32[]{:S(2)}) collective-permute-start(f32[13,16,128]{2,1,0:T(8,128)S(1)} %get-tuple-element.35), channel_id=1, source_target_pairs={{0,8},{8,16},{16,24},{24,28},{28,20},{20,12},{12,4},{4,5},{5,13},{... | collective-permute-start | bytes 319496 | tf_op jit(solution)/shard_map/ppermute | solution.py:993
  64.3 23.8 %collective-permute-start.3 = (f32[13,16,128]{2,1,0:T(8,128)S(1)}, f32[13,16,128]{2,1,0:T(8,128)S(1)}, u32[]{:S(2)}, u32[]{:S(2)}) collective-permute-start(f32[13,16,128]{2,1,0:T(8,128)S(1)} %get-tuple-element.36), channel_id=1, source_target_pairs={{8,0},{16,8},{24,16},{28,24},{20,28},{12,20},{4,12},{5,4},{13,5},{... | collective-permute-start | bytes 319496 | tf_op jit(solution)/shard_map/ppermute | solution.py:993
  89.6 8.6 %all-to-all-start.3 = ((bf16[8,6,16,128]{3,2,1,0:T(8,128)(2,1)}), bf16[8,6,16,128]{3,2,1,0:T(8,128)(2,1)S(1)}, u32[]{:S(2)}, u32[]{:S(2)}) async-start(bf16[8,6,16,128]{3,2,1,0:T(8,128)(2,1)} %get-tuple-element.39), calls=%async_computation.3 | async-start | bytes 393216 | tf_op jit(solution)/shard_map/all_to_all | solution.py:978
  94.6 8.8 %copy-start = (bf16[27,32]{1,0:T(8,128)(2,1)S(1)}, bf16[27,32]{1,0:T(8,128)(2,1)}, u32[]{:S(2)}) copy-start(bf16[27,32]{1,0:T(8,128)(2,1)} %w_ref.1) | copy-start | bytes 5188
  100.8 10.4 %all-to-all-start.4 = ((f32[32,8,128]{2,1,0:T(8,128)}), f32[32,8,128]{2,1,0:T(8,128)S(1)}, u32[]{:S(2)}, u32[]{:S(2)}) async-start(f32[32,8,128]{2,1,0:T(8,128)} %get-tuple-element.41.after_ref), calls=%async_computation.4 | async-start | bytes 262144 | tf_op jit(solution)/shard_map/all_to_all | solution.py:981
